TPU v7x, 768 devices: a whole 4x8x12 slice. The times are simulated.
768 devices in a mesh: band: 48 (over x, z), fld: 16 (over y, core).
Axes of the slice: x: 4, y: 8, z: 12, core: 2. Of those that a mesh axis runs over, the one named last changes fastest.
Arguments:
- grid_fields: bfloat16 [32, 2, 768, 3072], P('fld', None, 'band'), may hold values from -6 to 6
- legendre: bfloat16 [768, 2, 768, 513], P(('band', 'fld')), may hold values from -0.21875 to 0.21875
- slot_wave: int32 [1536], P(('band', 'fld')), may hold values from 0 to 1024, as said below
Outputs:
- spectrum: bfloat16 [768, 2, 32, 2, 513], P(('band', 'fld'))
Inputs may be any that keep to these rules, and one draw needn't show every extreme that they name: `slot_wave`: for every q, slots 2 q and 2 q + 1 hold m and 1023 - m for some m below 512, or both hold 1024; every wavenumber below 1024 is held by exactly one slot.
All inputs are finite; a program needn't handle non-finite values.
Results may differ from a plain program's by a relative error of at most 0.0059.
Values may be sent and summed in bfloat16 or wider, within the bound.
A program may use at most 32 MiB of HBM per device.

v0:
```python
import math

import jax
import jax.numpy as jnp
from jax import lax
from jax.sharding import Mesh
from jax.sharding import PartitionSpec as P

MM = 1024
BAND_FLD = ("band_0", "band_1", "fld_0", "fld_1")
BAND = ("band_0", "band_1")
FLD = ("fld_0", "fld_1")


def laid_out(pieces, dim):
    shape = list(pieces.shape[1:])
    shape[dim] *= pieces.shape[0]
    return jnp.moveaxis(pieces, 0, dim).reshape(shape)


def stacked_from(x, axes, turns):
    pieces = x[None]
    for k in turns:
        pieces = lax.all_gather(pieces, axes[k], axis=0, tiled=True)
    carried = [lax.axis_size(axes[k]) for k in reversed(turns)]
    pieces = pieces.reshape(*carried, *x.shape)
    turned = sorted(range(len(turns)), key=lambda place: turns[len(turns) - 1 - place])
    return pieces.transpose(*turned, *range(len(turns), pieces.ndim)).reshape(-1, *x.shape)


def whole_of(x, axes, turns, dim):
    return laid_out(stacked_from(x, axes, turns), dim)


def slot_table(wave_list, lon_count):
    lon_index = lax.broadcasted_iota(jnp.int32, (lon_count, wave_list.shape[0]), 0)
    phase_index = lon_index * wave_list[None, :] % lon_count
    phase_angle = phase_index.astype(jnp.float32) * (2.0 * math.pi / lon_count)
    norm_scale = 1.0 / math.sqrt(lon_count)
    live_mask = (wave_list < MM)[None, :]
    cosine = jnp.where(live_mask, jnp.cos(phase_angle) * norm_scale, 0.0)
    sine_part = jnp.where(live_mask, -jnp.sin(phase_angle) * norm_scale, 0.0)
    return jnp.stack([cosine, sine_part], axis=1).astype(jnp.bfloat16)


def local(grid_fields, legendre, slot_wave):
    wave_list = whole_of(slot_wave, BAND_FLD, (0, 2, 1, 3), 0)
    fields, hemispheres, lat_rows, lon_count = grid_fields.shape
    slot_count = wave_list.shape[0]
    blocks = max(1, slot_count // 256)
    grid_rows = grid_fields.reshape(fields * hemispheres * lat_rows, lon_count)

    def transform(block_waves):
        fourier_table = slot_table(block_waves, lon_count)
        return jnp.einsum(
            "al,lrs->ars", grid_rows, fourier_table, preferred_element_type=jnp.float32
        )

    blocks_out = lax.map(transform, wave_list.reshape(blocks, -1))
    fourier = jnp.moveaxis(blocks_out, 0, 2).reshape(fields, hemispheres, lat_rows, 2, slot_count)
    north_part = fourier[:, 0]
    south_part = fourier[:, 1]
    folded = jnp.stack([north_part + south_part, north_part - south_part], axis=1).astype(
        jnp.bfloat16
    )
    owner_data = lax.all_to_all(
        lax.all_to_all(folded, BAND, split_axis=4, concat_axis=2, tiled=True),
        FLD,
        split_axis=4,
        concat_axis=0,
        tiled=True,
    )
    total_fields, _, half_rows, _, own_slots = owner_data.shape
    pair_count = own_slots // 2
    paired = owner_data.reshape(total_fields, 2, half_rows, 2, pair_count, 2)
    products = jnp.einsum(
        "fphrqk,qphc->qpfrkc", paired, legendre, preferred_element_type=jnp.float32
    )
    own_waves = slot_wave.reshape(pair_count, 2)[:, 0]
    first_wave = own_waves[:, None, None]
    parity = lax.broadcasted_iota(jnp.int32, (1, 2, 1), 1)
    column = lax.broadcasted_iota(jnp.int32, (1, 1, legendre.shape[3]), 2)
    first_count = (MM - first_wave + 1 - parity) // 2
    second_count = (first_wave + 2 - parity) // 2
    first_mask = (column < first_count)[:, :, None, None, :]
    second_mask = ((column >= first_count) & (column < first_count + second_count))[
        :, :, None, None, :
    ]
    spectrum = jnp.where(
        first_mask, products[:, :, :, :, 0], jnp.where(second_mask, products[:, :, :, :, 1], 0.0)
    )
    return spectrum.astype(jnp.bfloat16)


def solution(mesh):
    finer = Mesh(mesh.devices.reshape(4, 12, 8, 2), ("band_0", "band_1", "fld_0", "fld_1"))
    placed = (P(FLD, None, BAND, None), P(BAND_FLD, None, None, None), P(BAND_FLD))
    return jax.shard_map(
        local,
        mesh=finer,
        in_specs=placed,
        out_specs=P(BAND_FLD, None, None, None, None),
        check_vma=False,
    )
```

profile of v0, /device:TPU:1, one launch (start us, length us, event | category | flops | bytes accessed | tf_op | source)
XLA Modules:
  0.0 225.6 jit_solution(8615979295264548961)
XLA Ops:
  0.0 0.0 copy-start
  0.0 1.4 dynamic-slice
  2.0 0.9 dynamic-update-slice
  2.8 7.7 %all-reduce = s32[8]{0:T(128)S(1)} all-reduce(s32[8]{0:T(128)S(1)} %dynamic-update-slice), channel_id=2, replica_groups=mesh['band_0'=4,'band_1'=12,'fld_0'=8,'fld_1'=2] {'band_0'}, use_global_device_ids=true, to_apply=%add | all-reduce | flops 8 | bytes 64
  10.5 0.1 reshape.384
  10.6 0.1 copy.19
  10.7 13.0 %all-gather.1 = s32[8,4,2]{1,2,0:T(2,128)S(1)} all-gather(s32[1,4,2]{1,2,0:T(2,128)S(1)} %copy.19), channel_id=1, replica_groups=mesh['band_0'=4,'band_1'=12,'fld_0'=8,'fld_1'=2] {'fld_0'}, dimensions={0}, use_global_device_ids=true | all-gather | bytes 288 | tf_op jit(solution)/shard_map/all_gather | solution.py:24
  23.7 0.1 reshape.386
  23.8 26.9 %all-gather.2 = s32[12,32,2]{1,2,0:T(2,128)S(1)} all-gather(s32[1,32,2]{1,2,0:T(2,128)S(1)} %reshape.386), channel_id=1, replica_groups=mesh['band_0'=4,'band_1'=12,'fld_0'=8,'fld_1'=2] {'band_1'}, dimensions={0}, use_global_device_ids=true | all-gather | bytes 3328 | tf_op jit(solution)/shard_map/all_gather | solution.py:24
  50.7 0.1 reshape.387
  50.8 13.3 %all_gather.15 = s32[768,2]{0,1:T(2,128)S(1)} all-gather(s32[384,2]{0,1:T(2,128)S(1)} %reshape.387), channel_id=1, replica_groups=mesh['band_0'=4,'band_1'=12,'fld_0'=8,'fld_1'=2] {'fld_1'}, dimensions={0}, use_global_device_ids=true | all-gather | bytes 9216 | tf_op jit(solution)/shard_map/all_gather | solution.py:24
  64.1 0.2 reshape.375
  64.3 1.5 copy.22
  65.8 0.5 reshape_reshape_reshape.3
  66.3 85.5 %while.12 = (s32[]{:T(128)}, f32[6,64,2,256]{3,1,2,0:T(8,128)S(1)}, s32[6,256]{1,0:T(8,128)S(1)}, bf16[64,3072]{1,0:T(8,128)(2,1)}, s32[]{:T(128)}) while((s32[]{:T(128)}, f32[6,64,2,256]{3,1,2,0:T(8,128)S(1)}, s32[6,256]{1,0:T(8,128)S(1)}, bf16[64,3072]{1,0:T(8,128)(2,1)}, s32[]{:T(128)}) %tuple.38), condition=%wide.region_1.2_spmd, body=%wide.region_0.1_spmd.sunk | while | flops 220201216 | bytes 8392297 | solution.py:59
  66.3 0.0 copy-start.1
  66.3 13.5 %select_convert_fusion.3 = (bf16[3072,1,256]{2,0,1:T(8,128)(2,1)S(1)}, bf16[3072,1,256]{2,0,1:T(8,128)(2,1)S(1)}) fusion(s32[256]{0:T(256)S(1)} %bitcast.71, pred[256]{0:T(512)(128)(4,1)S(1)} %get-tuple-element.108), kind=kLoop, calls=%fused_computation.8.clone.1 | loop fusion | flops 12582912 | bytes 3147008 | tf_op jit(solution)/shard_map/convert
  79.9 0.0 copy-done.1
  79.9 0.7 fusion.32
  80.6 0.0 copy-start.1
  80.6 13.5 %select_convert_fusion.3 = (bf16[3072,1,256]{2,0,1:T(8,128)(2,1)S(1)}, bf16[3072,1,256]{2,0,1:T(8,128)(2,1)S(1)}) fusion(s32[256]{0:T(256)S(1)} %bitcast.71, pred[256]{0:T(512)(128)(4,1)S(1)} %get-tuple-element.108), kind=kLoop, calls=%fused_computation.8.clone.1 | loop fusion | flops 12582912 | bytes 3147008 | tf_op jit(solution)/shard_map/convert
  94.1 0.0 copy-done.1
  94.1 0.7 fusion.32
  94.8 0.0 copy-start.1
  94.9 13.5 %select_convert_fusion.3 = (bf16[3072,1,256]{2,0,1:T(8,128)(2,1)S(1)}, bf16[3072,1,256]{2,0,1:T(8,128)(2,1)S(1)}) fusion(s32[256]{0:T(256)S(1)} %bitcast.71, pred[256]{0:T(512)(128)(4,1)S(1)} %get-tuple-element.108), kind=kLoop, calls=%fused_computation.8.clone.1 | loop fusion | flops 12582912 | bytes 3147008 | tf_op jit(solution)/shard_map/convert
  108.4 0.0 copy-done.1
  108.4 0.7 fusion.32
  109.1 0.0 copy-start.1
  109.1 13.5 %select_convert_fusion.3 = (bf16[3072,1,256]{2,0,1:T(8,128)(2,1)S(1)}, bf16[3072,1,256]{2,0,1:T(8,128)(2,1)S(1)}) fusion(s32[256]{0:T(256)S(1)} %bitcast.71, pred[256]{0:T(512)(128)(4,1)S(1)} %get-tuple-element.108), kind=kLoop, calls=%fused_computation.8.clone.1 | loop fusion | flops 12582912 | bytes 3147008 | tf_op jit(solution)/shard_map/convert
  122.6 0.0 copy-done.1
  122.6 0.7 fusion.32
  123.3 0.0 copy-start.1
  123.4 13.5 %select_convert_fusion.3 = (bf16[3072,1,256]{2,0,1:T(8,128)(2,1)S(1)}, bf16[3072,1,256]{2,0,1:T(8,128)(2,1)S(1)}) fusion(s32[256]{0:T(256)S(1)} %bitcast.71, pred[256]{0:T(512)(128)(4,1)S(1)} %get-tuple-element.108), kind=kLoop, calls=%fused_computation.8.clone.1 | loop fusion | flops 12582912 | bytes 3147008 | tf_op jit(solution)/shard_map/convert
  136.9 0.0 copy-done.1
  136.9 0.7 fusion.32
  137.6 0.0 copy-start.1
  137.6 13.5 %select_convert_fusion.3 = (bf16[3072,1,256]{2,0,1:T(8,128)(2,1)S(1)}, bf16[3072,1,256]{2,0,1:T(8,128)(2,1)S(1)}) fusion(s32[256]{0:T(256)S(1)} %bitcast.71, pred[256]{0:T(512)(128)(4,1)S(1)} %get-tuple-element.108), kind=kLoop, calls=%fused_computation.8.clone.1 | loop fusion | flops 12582912 | bytes 3147008 | tf_op jit(solution)/shard_map/convert
  151.1 0.0 copy-done.1
  151.1 0.7 fusion.32
  151.8 0.5 copy.23
  152.3 0.3 reshape.377
  152.6 0.1 add_convert_fusion
  152.7 5.5 %copy.24 = bf16[2,2,16,2,1536]{2,1,0,3,4:T(2,128)(2,1)} copy(bf16[2,2,16,2,1536]{4,2,1,0,3:T(8,128)(2,1)S(1)} %pad_maximum_fusion) | data formatting | bytes 786432 | tf_op jit(solution)/shard_map/stack | solution.py:63
  158.2 9.5 %reshape.395 = bf16[48,2,2048]{2,1,0:T(2,128)(2,1)S(1)} reshape(bf16[1536,2,2,2,16]{4,3,2,1,0:T(2,128)(2,1)} %bitcast.65) | data formatting | bytes 786432
  167.6 22.5 %all_to_all.33 = bf16[48,2,2048]{2,1,0:T(2,128)(2,1)S(1)} all-to-all(bf16[48,2,2048]{2,1,0:T(2,128)(2,1)S(1)} %reshape.395), channel_id=1, replica_groups=mesh['band_0'=4,'band_1'=12,'fld_0'=8,'fld_1'=2] {'band_0','band_1'}, dimensions={0} | all-to-all | bytes 786432 | tf_op jit(solution)/shard_map/all_to_all | solution.py:67
  190.1 3.4 %reshape.396 = bf16[1536,2,2,2,16]{4,3,2,1,0:T(2,128)(2,1)} reshape(bf16[48,2,2048]{2,1,0:T(2,128)(2,1)S(1)} %all_to_all.33) | data formatting | bytes 786432
  193.5 0.0 copy-start.2
  193.5 6.4 %copy.35 = bf16[2,2,16,2,48,32]{5,2,4,3,1,0:T(8,128)(2,1)S(1)} copy(bf16[2,2,16,2,48,32]{2,1,0,3,5,4:T(2,128)(2,1)} %bitcast.66) | data formatting | bytes 786432 | tf_op jit(solution)/shard_map/all_to_all | solution.py:67
  199.9 1.4 copy.27
  201.3 7.7 %all-to-all-start.1 = ((bf16[2,2,768,2,32]{2,3,1,0,4:T(2,128)(2,1)}), bf16[2,2,768,2,32]{2,3,1,0,4:T(2,128)(2,1)S(1)}, u32[]{:S(2)}, u32[]{:S(2)}) async-start(bf16[2,2,768,2,32]{2,3,1,0,4:T(2,128)(2,1)} %copy.27), calls=%async_computation.1 | async-start | bytes 786432 | tf_op jit(solution)/shard_map/all_to_all | solution.py:66
  209.0 0.0 copy-done.2
  209.1 0.1 iota_compare_fusion
  209.2 14.3 %all-to-all-done.1 = bf16[2,2,768,2,32]{2,3,1,0,4:T(2,128)(2,1)S(1)} async-done(((bf16[2,2,768,2,32]{2,3,1,0,4:T(2,128)(2,1)}), bf16[2,2,768,2,32]{2,3,1,0,4:T(2,128)(2,1)S(1)}, u32[]{:S(2)}, u32[]{:S(2)}) %all-to-all-start.1) | async-done | bytes 393248 | tf_op jit(solution)/shard_map/all_to_all | solution.py:66
  223.5 0.3 copy.29
  223.8 0.1 reshape.378
  224.0 0.0 copy-done
  224.0 0.7 fusion.19
  224.7 0.1 fusion.24
  224.8 0.8 copy.32
  (12 shorter events, 0.2 us)
Async XLA Ops:
  0.0 224.0 %copy-start = (bf16[1,2,768,513]{2,1,3,0:T(2,128)(2,1)S(1)}, bf16[1,2,768,513]{2,1,3,0:T(2,128)(2,1)}, u32[]{:S(2)}) copy-start(bf16[1,2,768,513]{2,1,3,0:T(2,128)(2,1)} %param.6) | copy-start | bytes 4727812
  66.3 13.6 %copy-start.1 = (bf16[64,3072]{1,0:T(8,128)(2,1)S(1)}, bf16[64,3072]{1,0:T(8,128)(2,1)}, u32[]{:S(2)}) copy-start(bf16[64,3072]{1,0:T(8,128)(2,1)} %get-tuple-element.124) | copy-start | bytes 1179652 | tf_op jit(solution)/shard_map/while
  80.6 13.6 %copy-start.1 = (bf16[64,3072]{1,0:T(8,128)(2,1)S(1)}, bf16[64,3072]{1,0:T(8,128)(2,1)}, u32[]{:S(2)}) copy-start(bf16[64,3072]{1,0:T(8,128)(2,1)} %get-tuple-element.124) | copy-start | bytes 1179652 | tf_op jit(solution)/shard_map/while
  94.8 13.6 %copy-start.1 = (bf16[64,3072]{1,0:T(8,128)(2,1)S(1)}, bf16[64,3072]{1,0:T(8,128)(2,1)}, u32[]{:S(2)}) copy-start(bf16[64,3072]{1,0:T(8,128)(2,1)} %get-tuple-element.124) | copy-start | bytes 1179652 | tf_op jit(solution)/shard_map/while
  109.1 13.6 %copy-start.1 = (bf16[64,3072]{1,0:T(8,128)(2,1)S(1)}, bf16[64,3072]{1,0:T(8,128)(2,1)}, u32[]{:S(2)}) copy-start(bf16[64,3072]{1,0:T(8,128)(2,1)} %get-tuple-element.124) | copy-start | bytes 1179652 | tf_op jit(solution)/shard_map/while
  123.3 13.6 %copy-start.1 = (bf16[64,3072]{1,0:T(8,128)(2,1)S(1)}, bf16[64,3072]{1,0:T(8,128)(2,1)}, u32[]{:S(2)}) copy-start(bf16[64,3072]{1,0:T(8,128)(2,1)} %get-tuple-element.124) | copy-start | bytes 1179652 | tf_op jit(solution)/shard_map/while
  137.6 13.6 %copy-start.1 = (bf16[64,3072]{1,0:T(8,128)(2,1)S(1)}, bf16[64,3072]{1,0:T(8,128)(2,1)}, u32[]{:S(2)}) copy-start(bf16[64,3072]{1,0:T(8,128)(2,1)} %get-tuple-element.124) | copy-start | bytes 1179652 | tf_op jit(solution)/shard_map/while
  193.5 15.6 %copy-start.2 = (s32[2]{0:T(128)S(1)}, s32[2]{0:T(128)}, u32[]{:S(2)}) copy-start(s32[2]{0:T(128)} %param.7) | copy-start | bytes 28
  201.3 22.2 %all-to-all-start.1 = ((bf16[2,2,768,2,32]{2,3,1,0,4:T(2,128)(2,1)}), bf16[2,2,768,2,32]{2,3,1,0,4:T(2,128)(2,1)S(1)}, u32[]{:S(2)}, u32[]{:S(2)}) async-start(bf16[2,2,768,2,32]{2,3,1,0,4:T(2,128)(2,1)} %copy.27), calls=%async_computation.1 | async-start | bytes 786432 | tf_op jit(solution)/shard_map/all_to_all | solution.py:66
where the time goes:
time: 226 us
  blocking collectives  83.4 us (37%)
  other arithmetic  81.5 us (36%)
  local copies, waits for them, and re-layouts  32.9 us (15%)
  waiting for transfers between devices  14.3 us (6%)
  starting transfers between devices  7.75 us (3%)
  matrix products  4.66 us (2%)
    another operation x7, other arithmetic  81.1 us
    all_gather x3, blocking collectives, stacked_from(): pieces = lax.all_gather(pieces, axes[k], axis=0, tiled=True)  53.2 us
    all_to_all x1, blocking collectives, local(): lax.all_to_all(folded, BAND, split_axis=4, concat_axis=2, tiled=True)  22.5 us
    unnamed x13, local copies, waits for them, and re-layouts  15.4 us
    all_to_all x1, waiting for transfers between devices, local(): lax.all_to_all(lax.all_to_all(folded, BAND, split_axis=4, concat_axis=2,...  14.3 us
    all_to_all x2, local copies, waits for them, and re-layouts, local(): lax.all_to_all(folded, BAND, split_axis=4, concat_axis=2, tiled=True)  7.79 us
    all_to_all x1, starting transfers between devices, local(): lax.all_to_all(lax.all_to_all(folded, BAND, split_axis=4, concat_axis=2,...  7.75 us
    unnamed x1, blocking collectives  7.68 us
  transfers between devices with their start and end apart: 1, of which 1 were waited for; matrix products, arithmetic and copies ran while one was open for 0% of the time, Pallas kernels for 0%

commit v1 on v0

v1 whole, which is shorter than its diff:
```python
import math

import jax
import jax.numpy as jnp
import numpy as np
from jax import lax
from jax.experimental import pallas as pl
from jax.experimental.pallas import tpu as pltpu
from jax.sharding import PartitionSpec as P

MM = 1024
NLON = 3072
INNER = 384
BANDS, FLDS = 48, 16
ZS = 12
STEPS = 16


def wave_rows(group, half):
    return group if half == 0 else (4 if group == 0 else 8 - group)


def table_seeds():
    waves = np.zeros((2, 4, 2, 64), np.int64)
    for s in range(2):
        for u in range(4):
            for half in range(2):
                waves[s, u, half] = wave_rows(u, half) + 8 * (64 * s + np.arange(64))
    waves = waves.reshape(1, 1024)
    rows = np.arange(STEPS).reshape(STEPS, 1)
    first = 2.0 * np.pi * ((rows * waves) % NLON) / NLON
    turn = np.broadcast_to(2.0 * np.pi * ((STEPS * waves) % NLON) / NLON, (STEPS, 1024))
    scale = 1.0 / math.sqrt(NLON)
    return np.stack([np.cos(first) * scale, np.sin(first) * scale, np.cos(turn), np.sin(turn)]).astype(np.float32)


def make_table(seeds, table):
    lane = lax.broadcasted_iota(jnp.int32, (STEPS, 128), 1)
    first_half = lane < 64
    for s in range(2):

        def rows(step, carry):
            at = pl.multiple_of(step * STEPS, STEPS)
            after = []
            for u in range(4):
                cosine, sine = carry[u]
                low, high = pl.ds(at, STEPS), pl.ds(at + INNER, STEPS)
                real, imag = pl.ds(s * 256, 128), pl.ds(s * 256 + 128, 128)
                if u == 0:
                    table[u, low, real] = jnp.where(first_half, cosine, 0.0).astype(jnp.bfloat16)
                    table[u, low, imag] = jnp.where(first_half, -sine, 0.0).astype(jnp.bfloat16)
                    table[u, high, real] = jnp.where(first_half, 0.0, cosine).astype(jnp.bfloat16)
                    table[u, high, imag] = jnp.where(first_half, 0.0, -sine).astype(jnp.bfloat16)
                else:
                    table[u, low, real] = cosine.astype(jnp.bfloat16)
                    table[u, low, imag] = (-sine).astype(jnp.bfloat16)
                    table[u, high, real] = jnp.where(first_half, sine, -sine).astype(jnp.bfloat16)
                    table[u, high, imag] = jnp.where(first_half, cosine, -cosine).astype(jnp.bfloat16)
                columns = pl.ds((s * 4 + u) * 128, 128)
                turn_cos, turn_sin = seeds[2, :, columns], seeds[3, :, columns]
                after.append((cosine * turn_cos - sine * turn_sin, sine * turn_cos + cosine * turn_sin))
            return tuple(after)

        start = tuple(
            (seeds[0, :, pl.ds((s * 4 + u) * 128, 128)], seeds[1, :, pl.ds((s * 4 + u) * 128, 128)]) for u in range(4)
        )
        lax.fori_loop(0, INNER // STEPS, rows, start)


def short_transform(grid, left):
    root = math.sqrt(0.5)
    for f in range(2):
        for block in range(3):
            north = [grid[f, 0, :, pl.ds(l * INNER + block * 128, 128)].astype(jnp.float32) for l in range(8)]
            south = [grid[f, 1, :, pl.ds(l * INNER + block * 128, 128)].astype(jnp.float32) for l in range(8)]
            for p in range(2):
                v = [a + b if p == 0 else a - b for a, b in zip(north, south, strict=True)]
                even = [v[l] + v[l + 4] for l in range(4)]
                odd = [v[l] - v[l + 4] for l in range(4)]
                minus = (odd[1] - odd[3]) * root
                plus = (odd[1] + odd[3]) * root
                pieces = (
                    ((even[0] + even[2]) + (even[1] + even[3]), (even[0] + even[2]) - (even[1] + even[3])),
                    (odd[0] + minus, -odd[2] - plus),
                    (even[0] - even[2], even[3] - even[1]),
                    (odd[0] - minus, odd[2] - plus),
                )
                for u in range(4):
                    for part in range(2):
                        left[u, pl.ds(f * 32 + p * 16, 16), pl.ds(part * INNER + block * 128, 128)] = pieces[u][
                            part
                        ].astype(jnp.bfloat16)


def long_transform(left, table, waves):
    for u in range(4):
        product = jnp.dot(left[u], table[u], preferred_element_type=jnp.float32)
        for s in range(2):
            for r in range(2):
                waves[s, pl.ds(r * 64, 64), pl.ds(u * 128, 128)] = product[
                    :, (s * 2 + r) * 128 : (s * 2 + r + 1) * 128
                ].astype(jnp.bfloat16)


def swap_groups(blocks, width):
    lane = lax.broadcasted_iota(jnp.int32, blocks[0].shape, 1)
    blocks = list(blocks)
    bit = 1
    while bit < len(blocks):
        shift = bit * width
        keep = (lane & shift) == 0
        for i in range(len(blocks)):
            if i & bit == 0:
                a, b = blocks[i], blocks[i + bit]
                blocks[i] = jnp.where(keep, a, pltpu.roll(b, shift, 1))
                blocks[i + bit] = jnp.where(keep, pltpu.roll(a, 128 - shift, 1), b)
        bit *= 2
    return blocks


def pick_slots(c, slot_rows, waves, one_hot, picked, outgoing):
    row = lax.broadcasted_iota(jnp.int32, (64, 128), 0) * 8
    for h in range(2):
        slots = jnp.broadcast_to(slot_rows[c, h : h + 1, :], (64, 128))
        for u in range(4):
            for half in range(2):
                here = row + wave_rows(u, half)
                place = (pl.ds(u * 128 + half * 64, 64), pl.ds(h * 128, 128))
                one_hot[(0, *place)] = jnp.where(here == slots, 1.0, 0.0).astype(jnp.bfloat16)
                one_hot[(1, *place)] = jnp.where(here == 511 - slots, 1.0, 0.0).astype(jnp.bfloat16)
    for s in range(2):
        picked[s] = jnp.dot(waves[s], one_hot[s], preferred_element_type=jnp.float32)
    for h in range(2):
        for part in range(2):
            blocks = [
                picked[g // 4, pl.ds((g % 4) * 32 + part * 16, 16), pl.ds(h * 128, 128)] for g in range(8)
            ]
            for k, block in enumerate(swap_groups(blocks, 1)):
                outgoing[h * 8 + k, c, pl.ds(part * 16, 16), :] = block.astype(jnp.bfloat16)


def gather_fields(c, arrived, turned):
    for part in range(2):
        blocks = [arrived[f, c, pl.ds(part * 16, 16), :].astype(jnp.float32) for f in range(FLDS)]
        for i, block in enumerate(swap_groups(blocks, 8)):
            turned[c, i, pl.ds(part * 16, 16), :] = block.astype(jnp.bfloat16)


def kernel(
    grid, slot, seeds, out,
    table, left, waves, one_hot, picked, outgoing, arrived, turned, own_column, all_slots, slot_rows,
    send_list, recv_list, send_lists, recv_lists, send_fld, recv_fld, send_band, recv_band,
):
    band, fld = lax.axis_index("band"), lax.axis_index("fld")
    x, z = band // ZS, band % ZS

    barrier = pltpu.get_barrier_semaphore()

    def greet(axis, me, size):
        def one(d, carry):
            pl.semaphore_signal(barrier, inc=1, device_id={axis: (me + d) % size})
            return carry

        lax.fori_loop(1, size, one, 0)

    greet("fld", fld, FLDS)
    greet("band", band, BANDS)

    make_table(seeds, table)
    short_transform(grid, left)
    own_column[fld] = jnp.full((1, 128), slot[0], jnp.int32)
    pl.semaphore_wait(barrier, FLDS - 1 + BANDS - 1)

    def list_copy(d, source):
        return pltpu.make_async_remote_copy(
            own_column.at[source], own_column.at[source], send_list.at[d], recv_list.at[d],
            device_id={"fld": (fld + d) % FLDS},
        )

    lax.fori_loop(1, FLDS, lambda d, k: (list_copy(d, fld).start(), k)[1], 0)
    long_transform(left, table, waves)
    lax.fori_loop(1, FLDS, lambda d, k: (list_copy(d, (fld + FLDS - d) % FLDS).wait_recv(), k)[1], 0)

    lane = lax.broadcasted_iota(jnp.int32, (1, 128), 1)
    for h in range(2):
        row = jnp.zeros((1, 128), jnp.int32)
        for k in range(8):
            row = row + jnp.where(lane % 8 == k, own_column[h * 8 + k], 0)
        all_slots[band, pl.ds(h, 1), :] = row

    def lists_copy(d, source):
        return pltpu.make_async_remote_copy(
            all_slots.at[source], all_slots.at[source], send_lists.at[d], recv_lists.at[d],
            device_id={"band": (band + d) % BANDS},
        )

    lax.fori_loop(1, BANDS, lambda d, k: (lists_copy(d, band).start(), k)[1], 0)
    lax.fori_loop(1, BANDS, lambda d, k: (lists_copy(d, (band + BANDS - d) % BANDS).wait_recv(), k)[1], 0)
    lanes = lax.broadcasted_iota(jnp.int32, (2, 128), 1)
    for c in range(3):
        rows = jnp.zeros((2, 128), jnp.int32)
        for i in range(16):
            rows = rows + jnp.where(lanes // 8 == i, all_slots[(i // 4) * ZS + (i % 4) * 3 + c], 0)
        slot_rows[c] = rows

    def fld_copy(step, c, d, source):
        return pltpu.make_async_remote_copy(
            outgoing.at[(fld + d) % FLDS, c], arrived.at[source, c], send_fld.at[step, d], recv_fld.at[step, d],
            device_id={"fld": (fld + d) % FLDS},
        )

    def chunk_out(step, carry):
        c = (z + step) % 3
        pick_slots(c, slot_rows, waves, one_hot, picked, outgoing)
        lax.fori_loop(1, FLDS, lambda d, k: (fld_copy(step, c, d, fld).start(), k)[1], 0)
        arrived[fld, c] = outgoing[fld, c]
        return carry

    lax.fori_loop(0, 3, chunk_out, 0)

    def band_copy(step, o, sign):
        dx, dz = o // 4, step + 3 * (o % 4)
        to_x, to_z = (x + dx) % 4, (z + dz) % ZS
        from_x, from_z = (x + 4 - dx) % 4, (z + ZS - dz) % ZS
        source = band if sign else from_x * ZS + from_z
        return pltpu.make_async_remote_copy(
            turned.at[to_z % 3, to_x * 4 + to_z // 3], out.at[source], send_band.at[step, o], recv_band.at[step, o],
            device_id={"band": to_x * ZS + to_z},
        )

    for step in range(3):
        c = (z + step) % 3
        lax.fori_loop(
            1, FLDS, lambda d, k: (fld_copy(step, c, d, (fld + FLDS - d) % FLDS).wait_recv(), k)[1], 0
        )
        gather_fields(c, arrived, turned)
        lax.fori_loop(0 if step else 1, 16, lambda o, k: (band_copy(step, o, True).start(), k)[1], 0)
        if step == 0:
            out[band] = turned[c, x * 4 + z // 3]
    for step in range(3):
        lax.fori_loop(0 if step else 1, 16, lambda o, k: (band_copy(step, o, False).wait_recv(), k)[1], 0)

    lax.fori_loop(1, FLDS, lambda d, k: (list_copy(d, fld).wait_send(), k)[1], 0)
    lax.fori_loop(1, BANDS, lambda d, k: (lists_copy(d, band).wait_send(), k)[1], 0)
    for step in range(3):
        c = (z + step) % 3
        lax.fori_loop(1, FLDS, lambda d, k: (fld_copy(step, c, d, fld).wait_send(), k)[1], 0)
        lax.fori_loop(0 if step else 1, 16, lambda o, k: (band_copy(step, o, True).wait_send(), k)[1], 0)


def folded_at_owner(grid_fields, slot_wave):
    bf16, f32, i32 = jnp.bfloat16, jnp.float32, jnp.int32
    vmem = pl.BlockSpec(memory_space=pltpu.VMEM)
    dma = pltpu.SemaphoreType.DMA
    return pl.pallas_call(
        kernel,
        out_shape=jax.ShapeDtypeStruct((BANDS, 32, 128), bf16),
        in_specs=[vmem, pl.BlockSpec(memory_space=pltpu.SMEM), vmem],
        out_specs=vmem,
        scratch_shapes=[
            pltpu.VMEM((4, 768, 512), bf16),
            pltpu.VMEM((4, 64, 768), bf16),
            pltpu.VMEM((2, 128, 512), bf16),
            pltpu.VMEM((2, 512, 256), bf16),
            pltpu.VMEM((2, 128, 256), f32),
            pltpu.VMEM((FLDS, 3, 32, 128), bf16),
            pltpu.VMEM((FLDS, 3, 32, 128), bf16),
            pltpu.VMEM((3, 16, 32, 128), bf16),
            pltpu.VMEM((FLDS, 1, 128), i32),
            pltpu.VMEM((BANDS, 2, 128), i32),
            pltpu.VMEM((3, 2, 128), i32),
            dma((FLDS,)), dma((FLDS,)), dma((BANDS,)), dma((BANDS,)),
            dma((3, FLDS)), dma((3, FLDS)), dma((3, 16)), dma((3, 16)),
        ],
        compiler_params=pltpu.CompilerParams(collective_id=0, has_side_effects=True),
        name="folded_at_owner",
    )(grid_fields, slot_wave, jnp.asarray(table_seeds()))


def local(grid_fields, legendre, slot_wave):
    folded = folded_at_owner(grid_fields, slot_wave)
    folded = folded.reshape(BANDS, 2, 16, 128)
    table = legendre[0].reshape(2, BANDS, 16, legendre.shape[3])
    products = jnp.einsum("bpjn,pbjc->pnc", folded, table, preferred_element_type=jnp.float32)
    products = products.reshape(2, 16, 2, 2, 2, legendre.shape[3])
    parity = lax.broadcasted_iota(jnp.int32, (2, legendre.shape[3]), 0)
    column = lax.broadcasted_iota(jnp.int32, (2, legendre.shape[3]), 1)
    first_count = (MM - slot_wave[0] + 1 - parity) // 2
    second_count = (slot_wave[0] + 2 - parity) // 2
    first_mask = (column < first_count)[:, None, None, None, :]
    second_mask = ((column >= first_count) & (column < first_count + second_count))[:, None, None, None, :]
    spectrum = jnp.where(first_mask, products[:, :, 0], jnp.where(second_mask, products[:, :, 1], 0.0))
    spectrum = spectrum.astype(jnp.bfloat16).transpose(0, 1, 3, 2, 4)
    return spectrum.reshape(1, 2, 32, 2, legendre.shape[3])


def solution(mesh):
    placed = (P("fld", None, "band", None), P(("band", "fld"), None, None, None), P(("band", "fld")))
    return jax.shard_map(
        local,
        mesh=mesh,
        in_specs=placed,
        out_specs=P(("band", "fld"), None, None, None, None),
        check_vma=False,
    )
```

time: 226 us -> 69.7 us (0.31)
  blocking collectives: 83.4 us -> 0 us
  other arithmetic: 81.5 us -> 0.34 us
  Pallas kernels: 0 us -> 62.7 us
  local copies, waits for them, and re-layouts: 32.9 us -> 5.41 us
  waiting for transfers between devices: 14.3 us -> 0 us
  starting transfers between devices: 7.75 us -> 0 us
  matrix products: 4.66 us -> 0.83 us
    another operation x8 -> x0, other arithmetic: 81.2 us -> none
    pallas_call x0 -> x1, Pallas kernels: none -> 62.7 us  [folded_at_owner(): pl.pallas_call(kernel, out_shape=jax.ShapeDtypeStruct((BANDS, 32, 128), b...]
    all_gather x3 -> x0, blocking collectives: 53.2 us -> none  [stacked_from(): pieces = lax.all_gather(pieces, axes[k], axis=0, tiled=True)]
    all_to_all x1 -> x0, blocking collectives: 22.5 us -> none  [local(): lax.all_to_all(folded, BAND, split_axis=4, concat_axis=2, tiled=True)]
    all_to_all x1 -> x0, waiting for transfers between devices: 14.3 us -> none  [local(): lax.all_to_all(lax.all_to_all(folded, BAND, split_axis=4, concat_axis=2,...]
    unnamed x13 -> x5, local copies, waits for them, and re-layouts: 15.4 us -> 3.88 us
    all_to_all x3 -> x0, local copies, waits for them, and re-layouts: 8.1 us -> none  [the longest x2 7.79 us: local(): lax.all_to_all(folded, BAND, split_axis=4, concat_axis=2, tiled=True)]
    all_to_all x1 -> x0, starting transfers between devices: 7.75 us -> none  [local(): lax.all_to_all(lax.all_to_all(folded, BAND, split_axis=4, concat_axis=2,...]
  transfers between devices with their start and end apart: 1 -> 0, of which waited for: 1 -> 0; matrix products, arithmetic and copies ran while one was open for 0% -> 0% of each run, Pallas kernels for 0% -> 0%
where the time goes in v1:
time: 69.7 us; the launch traced here: 69.5 us
  Pallas kernels  62.7 us (90%)
  local copies, waits for them, and re-layouts  5.41 us (8%)
  matrix products  0.83 us (1%)
    pallas_call x1, Pallas kernels, folded_at_owner(): pl.pallas_call(kernel, out_shape=jax.ShapeDtypeStruct((BANDS, 32, 128), b...  62.7 us
    unnamed x5, local copies, waits for them, and re-layouts  3.88 us

profile of v1, /device:TPU:1, one launch (start us, length us, event | category | flops | bytes accessed | tf_op | source)
XLA Modules:
  0.0 69.5 jit_solution(16102940036861516567)
XLA Ops:
  0.0 62.7 %folded_at_owner.1 = bf16[48,32,128]{2,1,0:T(8,128)(2,1)} custom-call(bf16[2,2,16,3072]{3,2,1,0:T(8,128)(2,1)} %grid.1, s32[2]{0:T(128)} %slot.1, f32[4,16,1024]{2,1,0:T(8,128)} %constant.38.clone.seeds), custom_call_target="tpu_custom_call" | custom-call | tf_op jit(solution)/shard_map/folded_at_owner/pallas_call | solution.py:255
  62.7 0.0 copy-start
  62.7 3.9 %copy.14 = bf16[1,2,768,513]{3,2,1,0:T(8,128)(2,1)S(1)} copy(bf16[1,2,768,513]{2,1,3,0:T(2,128)(2,1)} %param.5) | data formatting | bytes 3151872 | tf_op args[1]
  66.6 0.0 copy-start.1
  66.6 0.0 copy-done
  66.6 0.8 %fusion.2 = bf16[2,128,513]{1,2,0:T(8,128)(2,1)S(1)} fusion(bf16[48,2,16,128]{3,2,1,0:T(8,128)(2,1)S(1)} %bitcast.32, bf16[2,48,16,513]{3,2,1,0:T(8,128)(2,1)S(1)} %bitcast.30), kind=kOutput, calls=%fused_computation.2 | convolution fusion | flops 201719808 | bytes 2231808 | tf_op jit(solution)/shard_map/bpjn,pbjc->pnc/dot_general | solution.py:284
  67.5 0.7 %copy.16 = bf16[2,128,513]{2,0,1:T(2,128)(2,1)S(1)} copy(bf16[2,128,513]{1,2,0:T(8,128)(2,1)S(1)} %fusion.2) | data formatting | bytes 525312 | tf_op jit(solution)/shard_map/bpjn,pbjc->pnc/dot_general | solution.py:284
  68.2 0.0 copy-done.1
  68.3 0.1 select_compare_fusion
  68.4 0.2 fusion.8
  68.7 0.8 %copy.18 = bf16[2,16,2,2,513]{4,3,2,1,0:T(2,128)(2,1)} copy(bf16[2,16,2,2,513]{4,0,2,3,1:T(2,128)(2,1)S(1)} %fusion.8) | data formatting | bytes 262656 | tf_op jit(solution)/shard_map/transpose | solution.py:293
  (3 shorter events, 0.0 us)
Async XLA Ops:
  62.7 3.9 %copy-start = (bf16[48,32,128]{2,1,0:T(8,128)(2,1)S(1)}, bf16[48,32,128]{2,1,0:T(8,128)(2,1)}, u32[]{:S(2)}) copy-start(bf16[48,32,128]{2,1,0:T(8,128)(2,1)} %folded_at_owner.1) | copy-start | bytes 1179652
  66.6 1.6 %copy-start.1 = (s32[2]{0:T(128)S(1)}, s32[2]{0:T(128)}, u32[]{:S(2)}) copy-start(s32[2]{0:T(128)} %slot.1) | copy-start | bytes 28

commit v2 on v1

--- a/solution.py
+++ b/solution.py
@@ -141,45 +141,54 @@
 
 def gather_fields(c, arrived, turned):
     for part in range(2):
-        blocks = [arrived[f, c, pl.ds(part * 16, 16), :].astype(jnp.float32) for f in range(FLDS)]
+        blocks = [arrived[c, f, pl.ds(part * 16, 16), :].astype(jnp.float32) for f in range(FLDS)]
         for i, block in enumerate(swap_groups(blocks, 8)):
-            turned[c, i, pl.ds(part * 16, 16), :] = block.astype(jnp.bfloat16)
+            turned[c * 16 + i, pl.ds(part * 16, 16), :] = block.astype(jnp.bfloat16)
+
+
+def wrap(at, size):
+    return jnp.where(at >= size, at - size, at)
+
+
+def arrived_at(ref, semaphore):
+    pltpu.make_async_copy(ref, ref, semaphore).wait()
+
+
+def each(first, last, act):
+    lax.fori_loop(first, last, lambda k, carry: (act(k), carry)[1], 0)
 
 
 def kernel(
-    grid, slot, seeds, out,
-    table, left, waves, one_hot, picked, outgoing, arrived, turned, own_column, all_slots, slot_rows,
-    send_list, recv_list, send_lists, recv_lists, send_fld, recv_fld, send_band, recv_band,
+    grid_hbm, slot, seeds_hbm, out,
+    grid, seeds, table, left, waves, one_hot, picked, outgoing, arrived, turned, own_column, all_slots, slot_rows, by_row,
+    input_sem, send_list, recv_list, send_lists, recv_lists, send_fld, recv_fld, send_band, recv_band,
 ):
     band, fld = lax.axis_index("band"), lax.axis_index("fld")
     x, z = band // ZS, band % ZS
+    inputs = (
+        pltpu.make_async_copy(seeds_hbm, seeds, input_sem.at[0]),
+        pltpu.make_async_copy(grid_hbm, grid, input_sem.at[1]),
+    )
 
     barrier = pltpu.get_barrier_semaphore()
-
-    def greet(axis, me, size):
-        def one(d, carry):
-            pl.semaphore_signal(barrier, inc=1, device_id={axis: (me + d) % size})
-            return carry
-
-        lax.fori_loop(1, size, one, 0)
-
-    greet("fld", fld, FLDS)
-    greet("band", band, BANDS)
-
+    each(1, BANDS, lambda d: pl.semaphore_signal(barrier, inc=1, device_id={"band": wrap(band + d, BANDS)}))
+    each(1, FLDS, lambda d: pl.semaphore_signal(barrier, inc=1, device_id={"fld": wrap(fld + d, FLDS)}))
+    for copy in inputs:
+        copy.start()
+    own_column[fld] = jnp.full((1, 128), slot[0], jnp.int32)
+    pl.semaphore_wait(barrier, FLDS - 1 + BANDS - 1)
+
+    def list_start(d):
+        pltpu.make_async_remote_copy(
+            own_column.at[fld], own_column.at[fld], send_list, recv_list, device_id={"fld": wrap(fld + d, FLDS)}
+        ).start()
+
+    each(1, FLDS, list_start)
+    for copy in inputs:
+        copy.wait()
     make_table(seeds, table)
     short_transform(grid, left)
-    own_column[fld] = jnp.full((1, 128), slot[0], jnp.int32)
-    pl.semaphore_wait(barrier, FLDS - 1 + BANDS - 1)
-
-    def list_copy(d, source):
-        return pltpu.make_async_remote_copy(
-            own_column.at[source], own_column.at[source], send_list.at[d], recv_list.at[d],
-            device_id={"fld": (fld + d) % FLDS},
-        )
-
-    lax.fori_loop(1, FLDS, lambda d, k: (list_copy(d, fld).start(), k)[1], 0)
-    long_transform(left, table, waves)
-    lax.fori_loop(1, FLDS, lambda d, k: (list_copy(d, (fld + FLDS - d) % FLDS).wait_recv(), k)[1], 0)
+    arrived_at(own_column.at[pl.ds(0, FLDS - 1)], recv_list)
 
     lane = lax.broadcasted_iota(jnp.int32, (1, 128), 1)
     for h in range(2):
@@ -188,14 +197,14 @@
             row = row + jnp.where(lane % 8 == k, own_column[h * 8 + k], 0)
         all_slots[band, pl.ds(h, 1), :] = row
 
-    def lists_copy(d, source):
-        return pltpu.make_async_remote_copy(
-            all_slots.at[source], all_slots.at[source], send_lists.at[d], recv_lists.at[d],
-            device_id={"band": (band + d) % BANDS},
-        )
-
-    lax.fori_loop(1, BANDS, lambda d, k: (lists_copy(d, band).start(), k)[1], 0)
-    lax.fori_loop(1, BANDS, lambda d, k: (lists_copy(d, (band + BANDS - d) % BANDS).wait_recv(), k)[1], 0)
+    def lists_start(d):
+        pltpu.make_async_remote_copy(
+            all_slots.at[band], all_slots.at[band], send_lists, recv_lists, device_id={"band": wrap(band + d, BANDS)}
+        ).start()
+
+    each(1, BANDS, lists_start)
+    long_transform(left, table, waves)
+    arrived_at(all_slots.at[pl.ds(0, BANDS - 1)], recv_lists)
     lanes = lax.broadcasted_iota(jnp.int32, (2, 128), 1)
     for c in range(3):
         rows = jnp.zeros((2, 128), jnp.int32)
@@ -203,74 +212,71 @@
             rows = rows + jnp.where(lanes // 8 == i, all_slots[(i // 4) * ZS + (i % 4) * 3 + c], 0)
         slot_rows[c] = rows
 
-    def fld_copy(step, c, d, source):
-        return pltpu.make_async_remote_copy(
-            outgoing.at[(fld + d) % FLDS, c], arrived.at[source, c], send_fld.at[step, d], recv_fld.at[step, d],
-            device_id={"fld": (fld + d) % FLDS},
-        )
+    def fld_start(step, c, d):
+        to = wrap(fld + d, FLDS)
+        pltpu.make_async_remote_copy(
+            outgoing.at[to, c], arrived.at[c, fld], send_fld, recv_fld.at[step], device_id={"fld": to}
+        ).start()
 
     def chunk_out(step, carry):
         c = (z + step) % 3
         pick_slots(c, slot_rows, waves, one_hot, picked, outgoing)
-        lax.fori_loop(1, FLDS, lambda d, k: (fld_copy(step, c, d, fld).start(), k)[1], 0)
-        arrived[fld, c] = outgoing[fld, c]
+        each(1, FLDS, lambda d: fld_start(step, c, d))
+        arrived[c, fld] = outgoing[fld, c]
         return carry
 
     lax.fori_loop(0, 3, chunk_out, 0)
 
-    def band_copy(step, o, sign):
-        dx, dz = o // 4, step + 3 * (o % 4)
-        to_x, to_z = (x + dx) % 4, (z + dz) % ZS
-        from_x, from_z = (x + 4 - dx) % 4, (z + ZS - dz) % ZS
-        source = band if sign else from_x * ZS + from_z
-        return pltpu.make_async_remote_copy(
-            turned.at[to_z % 3, to_x * 4 + to_z // 3], out.at[source], send_band.at[step, o], recv_band.at[step, o],
+    def band_start(step, o):
+        to_x, to_z = wrap(x + o // 4, 4), wrap(z + step + 3 * (o % 4), ZS)
+        pltpu.make_async_remote_copy(
+            turned.at[(to_z % 3) * 16 + to_x * 4 + to_z // 3], by_row.at[band], send_band, recv_band,
             device_id={"band": to_x * ZS + to_z},
-        )
+        ).start()
 
     for step in range(3):
         c = (z + step) % 3
-        lax.fori_loop(
-            1, FLDS, lambda d, k: (fld_copy(step, c, d, (fld + FLDS - d) % FLDS).wait_recv(), k)[1], 0
-        )
+        arrived_at(arrived.at[c, pl.ds(0, FLDS - 1)], recv_fld.at[step])
         gather_fields(c, arrived, turned)
-        lax.fori_loop(0 if step else 1, 16, lambda o, k: (band_copy(step, o, True).start(), k)[1], 0)
+        each(0 if step else 1, 16, lambda o: band_start(step, o))
         if step == 0:
-            out[band] = turned[c, x * 4 + z // 3]
-    for step in range(3):
-        lax.fori_loop(0 if step else 1, 16, lambda o, k: (band_copy(step, o, False).wait_recv(), k)[1], 0)
-
-    lax.fori_loop(1, FLDS, lambda d, k: (list_copy(d, fld).wait_send(), k)[1], 0)
-    lax.fori_loop(1, BANDS, lambda d, k: (lists_copy(d, band).wait_send(), k)[1], 0)
-    for step in range(3):
-        c = (z + step) % 3
-        lax.fori_loop(1, FLDS, lambda d, k: (fld_copy(step, c, d, fld).wait_send(), k)[1], 0)
-        lax.fori_loop(0 if step else 1, 16, lambda o, k: (band_copy(step, o, True).wait_send(), k)[1], 0)
+            by_row[band] = turned[c * 16 + x * 4 + z // 3]
+    arrived_at(own_column.at[pl.ds(0, FLDS - 1)], send_list)
+    arrived_at(all_slots.at[pl.ds(0, BANDS - 1)], send_lists)
+    arrived_at(outgoing.at[pl.ds(0, FLDS - 1)], send_fld)
+    arrived_at(by_row.at[pl.ds(0, BANDS - 1)], recv_band)
+    for p in range(2):
+        for block in range(6):
+            rows = by_row[pl.ds(block * 8, 8), pl.ds(p * 16, 16), :].reshape(128, 128)
+            out[p, :, pl.ds(block * 128, 128)] = rows.T
+    arrived_at(turned.at[pl.ds(0, BANDS - 1)], send_band)
 
 
 def folded_at_owner(grid_fields, slot_wave):
     bf16, f32, i32 = jnp.bfloat16, jnp.float32, jnp.int32
-    vmem = pl.BlockSpec(memory_space=pltpu.VMEM)
+    any_space = pl.BlockSpec(memory_space=pl.ANY)
     dma = pltpu.SemaphoreType.DMA
     return pl.pallas_call(
         kernel,
-        out_shape=jax.ShapeDtypeStruct((BANDS, 32, 128), bf16),
-        in_specs=[vmem, pl.BlockSpec(memory_space=pltpu.SMEM), vmem],
-        out_specs=vmem,
+        out_shape=jax.ShapeDtypeStruct((2, 128, BANDS * 16), bf16),
+        in_specs=[any_space, pl.BlockSpec(memory_space=pltpu.SMEM), any_space],
+        out_specs=pl.BlockSpec(memory_space=pltpu.VMEM),
         scratch_shapes=[
+            pltpu.VMEM(grid_fields.shape, bf16),
+            pltpu.VMEM((4, STEPS, 1024), f32),
             pltpu.VMEM((4, 768, 512), bf16),
             pltpu.VMEM((4, 64, 768), bf16),
             pltpu.VMEM((2, 128, 512), bf16),
             pltpu.VMEM((2, 512, 256), bf16),
             pltpu.VMEM((2, 128, 256), f32),
             pltpu.VMEM((FLDS, 3, 32, 128), bf16),
-            pltpu.VMEM((FLDS, 3, 32, 128), bf16),
-            pltpu.VMEM((3, 16, 32, 128), bf16),
+            pltpu.VMEM((3, FLDS, 32, 128), bf16),
+            pltpu.VMEM((BANDS, 32, 128), bf16),
             pltpu.VMEM((FLDS, 1, 128), i32),
             pltpu.VMEM((BANDS, 2, 128), i32),
             pltpu.VMEM((3, 2, 128), i32),
-            dma((FLDS,)), dma((FLDS,)), dma((BANDS,)), dma((BANDS,)),
-            dma((3, FLDS)), dma((3, FLDS)), dma((3, 16)), dma((3, 16)),
+            pltpu.VMEM((BANDS, 32, 128), bf16),
+            dma((2,)), dma, dma, dma, dma, dma, dma((3,)), dma, dma,
         ],
         compiler_params=pltpu.CompilerParams(collective_id=0, has_side_effects=True),
         name="folded_at_owner",
@@ -279,9 +285,7 @@
 
 def local(grid_fields, legendre, slot_wave):
     folded = folded_at_owner(grid_fields, slot_wave)
-    folded = folded.reshape(BANDS, 2, 16, 128)
-    table = legendre[0].reshape(2, BANDS, 16, legendre.shape[3])
-    products = jnp.einsum("bpjn,pbjc->pnc", folded, table, preferred_element_type=jnp.float32)
+    products = jnp.einsum("pnj,pjc->pnc", folded, legendre[0], preferred_element_type=jnp.float32)
     products = products.reshape(2, 16, 2, 2, 2, legendre.shape[3])
     parity = lax.broadcasted_iota(jnp.int32, (2, legendre.shape[3]), 0)
     column = lax.broadcasted_iota(jnp.int32, (2, legendre.shape[3]), 1)

time: 69.7 us -> 62.8 us (0.901)
  local copies, waits for them, and re-layouts: 5.41 us -> 1.54 us
  Pallas kernels: 62.7 us -> 59.1 us
  matrix products: 0.83 us -> 1.58 us
    unnamed x5 -> x4, local copies, waits for them, and re-layouts: 3.88 us -> 0.01 us
    pallas_call x1, Pallas kernels: 62.7 us -> 59.1 us  [folded_at_owner(): pl.pallas_call(kernel, out_shape=jax.ShapeDtypeStruct((2, 128, BANDS * 16...]
    dot_general x1, matrix products: 0.83 us -> 1.58 us  [local(): jnp.einsum('pnj,pjc->pnc', folded, legendre[0], preferred_element_type=jn...]
where the time goes in v2:
time: 62.8 us; the launch traced here: 62.7 us
  Pallas kernels  59.1 us (94%)
  matrix products  1.58 us (3%)
  local copies, waits for them, and re-layouts  1.54 us (2%)
    pallas_call x1, Pallas kernels, folded_at_owner(): pl.pallas_call(kernel, out_shape=jax.ShapeDtypeStruct((2, 128, BANDS * 16...  59.1 us
    dot_general x1, matrix products, local(): jnp.einsum('pnj,pjc->pnc', folded, legendre[0], preferred_element_type=jn...  1.58 us

profile of v2, /device:TPU:1, one launch (start us, length us, event | category | flops | bytes accessed | tf_op | source)
XLA Modules:
  0.0 62.7 jit_solution(11909189054246691553)
XLA Ops:
  0.0 0.0 copy-start
  0.0 59.1 %folded_at_owner.1 = bf16[2,128,768]{2,1,0:T(8,128)(2,1)} custom-call(bf16[2,2,16,3072]{3,2,1,0:T(8,128)(2,1)} %grid_hbm.1, s32[2]{0:T(128)} %slot.1, f32[4,16,1024]{2,1,0:T(8,128)} %constant.38.clone.seeds_hbm), custom_call_target="tpu_custom_call" | custom-call | tf_op jit(solution)/shard_map/folded_at_owner/pallas_call | solution.py:259
  59.1 0.0 copy-done
  59.1 0.0 copy-start.1
  59.1 1.6 %fusion = bf16[2,128,513]{1,2,0:T(8,128)(2,1)S(1)} fusion(bf16[2,128,768]{2,1,0:T(8,128)(2,1)} %folded_at_owner.1, bf16[2,768,513]{1,0,2:T(2,128)(2,1)S(1)} %bitcast.27), kind=kOutput, calls=%fused_computation | convolution fusion | flops 201719808 | bytes 2231808 | tf_op jit(solution)/shard_map/pnj,pjc->pnc/dot_general | solution.py:288
  60.7 0.7 %copy.12 = bf16[2,128,513]{2,0,1:T(2,128)(2,1)S(1)} copy(bf16[2,128,513]{1,2,0:T(8,128)(2,1)S(1)} %fusion) | data formatting | bytes 525312 | tf_op jit(solution)/shard_map/pnj,pjc->pnc/dot_general | solution.py:288
  61.4 0.0 copy-done.1
  61.6 0.1 select_compare_fusion
  61.7 0.2 fusion.5
  61.9 0.8 %copy.14 = bf16[2,16,2,2,513]{4,3,2,1,0:T(2,128)(2,1)} copy(bf16[2,16,2,2,513]{4,0,2,3,1:T(2,128)(2,1)S(1)} %fusion.5) | data formatting | bytes 262656 | tf_op jit(solution)/shard_map/transpose | solution.py:297
  (3 shorter events, 0.0 us)
Async XLA Ops:
  0.0 59.1 %copy-start = (bf16[1,2,768,513]{2,1,3,0:T(2,128)(2,1)S(1)}, bf16[1,2,768,513]{2,1,3,0:T(2,128)(2,1)}, u32[]{:S(2)}) copy-start(bf16[1,2,768,513]{2,1,3,0:T(2,128)(2,1)} %param.5) | copy-start | bytes 4727812
  59.1 2.3 %copy-start.1 = (s32[2]{0:T(128)S(1)}, s32[2]{0:T(128)}, u32[]{:S(2)}) copy-start(s32[2]{0:T(128)} %slot.1) | copy-start | bytes 28

commit v3 on v2

--- a/solution.py
+++ b/solution.py
@@ -102,19 +102,17 @@
                 ].astype(jnp.bfloat16)
 
 
-def swap_groups(blocks, width):
+def swap_groups(blocks, shifts):
     lane = lax.broadcasted_iota(jnp.int32, blocks[0].shape, 1)
     blocks = list(blocks)
-    bit = 1
-    while bit < len(blocks):
-        shift = bit * width
+    for place, shift in enumerate(shifts):
+        bit = 1 << place
         keep = (lane & shift) == 0
         for i in range(len(blocks)):
             if i & bit == 0:
                 a, b = blocks[i], blocks[i + bit]
                 blocks[i] = jnp.where(keep, a, pltpu.roll(b, shift, 1))
                 blocks[i + bit] = jnp.where(keep, pltpu.roll(a, 128 - shift, 1), b)
-        bit *= 2
     return blocks
 
 
@@ -133,17 +131,42 @@
     for h in range(2):
         for part in range(2):
             blocks = [
-                picked[g // 4, pl.ds((g % 4) * 32 + part * 16, 16), pl.ds(h * 128, 128)] for g in range(8)
+                picked[g // 4, pl.ds((g % 2) * 64 + (g // 2 % 2) * 32 + part * 16, 16), pl.ds(h * 128, 128)]
+                for g in range(8)
             ]
-            for k, block in enumerate(swap_groups(blocks, 1)):
+            for k, block in enumerate(swap_groups(blocks, (1, 2, 64))):
                 outgoing[h * 8 + k, c, pl.ds(part * 16, 16), :] = block.astype(jnp.bfloat16)
 
 
 def gather_fields(c, arrived, turned):
     for part in range(2):
         blocks = [arrived[c, f, pl.ds(part * 16, 16), :].astype(jnp.float32) for f in range(FLDS)]
-        for i, block in enumerate(swap_groups(blocks, 8)):
+        for i, block in enumerate(swap_groups(blocks, (4, 8, 16, 32))):
             turned[c * 16 + i, pl.ds(part * 16, 16), :] = block.astype(jnp.bfloat16)
+
+
+def turn_legendre(legendre, by_j):
+    first = lax.broadcasted_iota(jnp.int32, (128, 128), 0) == 0
+    for block in range(6):
+        at = pl.ds(block * 128, 128)
+        for c in range(5):
+            if c < 4:
+                values = legendre[pl.ds(c * 128, 128), :, at].astype(jnp.float32)
+            else:
+                values = legendre[pl.ds(512, 1), :, at].astype(jnp.float32)
+            for p in range(2):
+                piece = values[:, p, :]
+                if c == 4:
+                    piece = jnp.where(first, jnp.broadcast_to(piece, (128, 128)), 0.0)
+                by_j[p, at, pl.ds(c * 128, 128)] = piece.astype(jnp.bfloat16).T
+
+
+def choose_columns(p, wave, products):
+    column = lax.broadcasted_iota(jnp.int32, (64, 640), 1)
+    first_count = (MM - wave + 1 - p) >> 1
+    second_count = (wave + 2 - p) >> 1
+    second = jnp.where(column < first_count + second_count, products[64:], 0.0)
+    return jnp.where(column < first_count, products[:64], second)
 
 
 def wrap(at, size):
@@ -159,8 +182,8 @@
 
 
 def kernel(
-    grid_hbm, slot, seeds_hbm, out,
-    grid, seeds, table, left, waves, one_hot, picked, outgoing, arrived, turned, own_column, all_slots, slot_rows, by_row,
+    grid_hbm, slot_hbm, seeds_hbm, legendre_hbm, out,
+    grid, slot, seeds, legendre, by_j, flipped, table, left, waves, one_hot, picked, outgoing, arrived, turned, own_column, all_slots, slot_rows, by_row,
     input_sem, send_list, recv_list, send_lists, recv_lists, send_fld, recv_fld, send_band, recv_band,
 ):
     band, fld = lax.axis_index("band"), lax.axis_index("fld")
@@ -168,13 +191,17 @@
     inputs = (
         pltpu.make_async_copy(seeds_hbm, seeds, input_sem.at[0]),
         pltpu.make_async_copy(grid_hbm, grid, input_sem.at[1]),
+        pltpu.make_async_copy(legendre_hbm, legendre, input_sem.at[2]),
     )
+    own_slot = pltpu.make_async_copy(slot_hbm, slot, input_sem.at[3])
+    own_slot.start()
 
     barrier = pltpu.get_barrier_semaphore()
     each(1, BANDS, lambda d: pl.semaphore_signal(barrier, inc=1, device_id={"band": wrap(band + d, BANDS)}))
     each(1, FLDS, lambda d: pl.semaphore_signal(barrier, inc=1, device_id={"fld": wrap(fld + d, FLDS)}))
     for copy in inputs:
         copy.start()
+    own_slot.wait()
     own_column[fld] = jnp.full((1, 128), slot[0], jnp.int32)
     pl.semaphore_wait(barrier, FLDS - 1 + BANDS - 1)
 
@@ -184,7 +211,7 @@
         ).start()
 
     each(1, FLDS, list_start)
-    for copy in inputs:
+    for copy in inputs[:2]:
         copy.wait()
     make_table(seeds, table)
     short_transform(grid, left)
@@ -194,7 +221,7 @@
     for h in range(2):
         row = jnp.zeros((1, 128), jnp.int32)
         for k in range(8):
-            row = row + jnp.where(lane % 8 == k, own_column[h * 8 + k], 0)
+            row = row + jnp.where(lane // 64 * 4 + lane % 4 == k, own_column[h * 8 + k], 0)
         all_slots[band, pl.ds(h, 1), :] = row
 
     def lists_start(d):
@@ -209,7 +236,7 @@
     for c in range(3):
         rows = jnp.zeros((2, 128), jnp.int32)
         for i in range(16):
-            rows = rows + jnp.where(lanes // 8 == i, all_slots[(i // 4) * ZS + (i % 4) * 3 + c], 0)
+            rows = rows + jnp.where(lanes // 4 % 16 == i, all_slots[(i // 4) * ZS + (i % 4) * 3 + c], 0)
         slot_rows[c] = rows
 
     def fld_start(step, c, d):
@@ -241,6 +268,8 @@
         each(0 if step else 1, 16, lambda o: band_start(step, o))
         if step == 0:
             by_row[band] = turned[c * 16 + x * 4 + z // 3]
+    inputs[2].wait()
+    turn_legendre(legendre, by_j)
     arrived_at(own_column.at[pl.ds(0, FLDS - 1)], send_list)
     arrived_at(all_slots.at[pl.ds(0, BANDS - 1)], send_lists)
     arrived_at(outgoing.at[pl.ds(0, FLDS - 1)], send_fld)
@@ -248,22 +277,30 @@
     for p in range(2):
         for block in range(6):
             rows = by_row[pl.ds(block * 8, 8), pl.ds(p * 16, 16), :].reshape(128, 128)
-            out[p, :, pl.ds(block * 128, 128)] = rows.T
+            flipped[p, :, pl.ds(block * 128, 128)] = rows.T
+    for p in range(2):
+        products = jnp.dot(flipped[p], by_j[p], preferred_element_type=jnp.float32)
+        out[p] = choose_columns(p, slot[0], products).astype(jnp.bfloat16).reshape(32, 2, 640)[:, :, :513]
     arrived_at(turned.at[pl.ds(0, BANDS - 1)], send_band)
 
 
-def folded_at_owner(grid_fields, slot_wave):
+def spectrum_at_owner(grid_fields, slot_wave, legendre):
     bf16, f32, i32 = jnp.bfloat16, jnp.float32, jnp.int32
-    any_space = pl.BlockSpec(memory_space=pl.ANY)
+    hbm = pl.BlockSpec(memory_space=pltpu.HBM)
     dma = pltpu.SemaphoreType.DMA
+    operands = grid_fields, slot_wave, jnp.asarray(table_seeds()), legendre
     return pl.pallas_call(
         kernel,
-        out_shape=jax.ShapeDtypeStruct((2, 128, BANDS * 16), bf16),
-        in_specs=[any_space, pl.BlockSpec(memory_space=pltpu.SMEM), any_space],
+        out_shape=jax.ShapeDtypeStruct((2, 32, 2, legendre.shape[0]), bf16),
+        in_specs=[hbm] * 4,
         out_specs=pl.BlockSpec(memory_space=pltpu.VMEM),
         scratch_shapes=[
             pltpu.VMEM(grid_fields.shape, bf16),
+            pltpu.SMEM((2,), i32),
             pltpu.VMEM((4, STEPS, 1024), f32),
+            pltpu.VMEM(legendre.shape, bf16),
+            pltpu.VMEM((2, 768, 640), bf16),
+            pltpu.VMEM((2, 128, 768), bf16),
             pltpu.VMEM((4, 768, 512), bf16),
             pltpu.VMEM((4, 64, 768), bf16),
             pltpu.VMEM((2, 128, 512), bf16),
@@ -276,26 +313,17 @@
             pltpu.VMEM((BANDS, 2, 128), i32),
             pltpu.VMEM((3, 2, 128), i32),
             pltpu.VMEM((BANDS, 32, 128), bf16),
-            dma((2,)), dma, dma, dma, dma, dma, dma((3,)), dma, dma,
+            dma((4,)), dma, dma, dma, dma, dma, dma((3,)), dma, dma,
         ],
-        compiler_params=pltpu.CompilerParams(collective_id=0, has_side_effects=True),
-        name="folded_at_owner",
-    )(grid_fields, slot_wave, jnp.asarray(table_seeds()))
+        compiler_params=pltpu.CompilerParams(
+            collective_id=0, has_side_effects=True, vmem_limit_bytes=24 * 1024 * 1024
+        ),
+        name="spectrum_at_owner",
+    )(*(pltpu.with_memory_space_constraint(a, pltpu.HBM) for a in operands))
 
 
 def local(grid_fields, legendre, slot_wave):
-    folded = folded_at_owner(grid_fields, slot_wave)
-    products = jnp.einsum("pnj,pjc->pnc", folded, legendre[0], preferred_element_type=jnp.float32)
-    products = products.reshape(2, 16, 2, 2, 2, legendre.shape[3])
-    parity = lax.broadcasted_iota(jnp.int32, (2, legendre.shape[3]), 0)
-    column = lax.broadcasted_iota(jnp.int32, (2, legendre.shape[3]), 1)
-    first_count = (MM - slot_wave[0] + 1 - parity) // 2
-    second_count = (slot_wave[0] + 2 - parity) // 2
-    first_mask = (column < first_count)[:, None, None, None, :]
-    second_mask = ((column >= first_count) & (column < first_count + second_count))[:, None, None, None, :]
-    spectrum = jnp.where(first_mask, products[:, :, 0], jnp.where(second_mask, products[:, :, 1], 0.0))
-    spectrum = spectrum.astype(jnp.bfloat16).transpose(0, 1, 3, 2, 4)
-    return spectrum.reshape(1, 2, 32, 2, legendre.shape[3])
+    return spectrum_at_owner(grid_fields, slot_wave, legendre[0].transpose(2, 0, 1))[None]
 
 
 def solution(mesh):

time: 62.8 us -> 58.8 us (0.936)
  matrix products: 1.58 us -> 0 us
  Pallas kernels: 59.1 us -> 58 us
  local copies, waits for them, and re-layouts: 1.54 us -> 0.67 us
    dot_general x1 -> x0, matrix products: 1.58 us -> none  [local(): jnp.einsum('pnj,pjc->pnc', folded, legendre[0], preferred_element_type=jn...]
    pallas_call x1, Pallas kernels: 59.1 us -> 58 us  [spectrum_at_owner(): pl.pallas_call(kernel, out_shape=jax.ShapeDtypeStruct((2, 32, 2, legendre...]
    transpose x1 -> x0, local copies, waits for them, and re-layouts: 0.79 us -> none  [local(): spectrum = spectrum.astype(jnp.bfloat16).transpose(0, 1, 3, 2, 4)]
    dot_general x1 -> x0, local copies, waits for them, and re-layouts: 0.74 us -> none  [local(): jnp.einsum('pnj,pjc->pnc', folded, legendre[0], preferred_element_type=jn...]
    unnamed x4 -> x1, local copies, waits for them, and re-layouts: 0.01 us -> 0.67 us
where the time goes in v3:
time: 58.8 us; the launch traced here: 58.7 us
  Pallas kernels  58 us (99%)
  local copies, waits for them, and re-layouts  0.67 us (1%)
    pallas_call x1, Pallas kernels, spectrum_at_owner(): pl.pallas_call(kernel, out_shape=jax.ShapeDtypeStruct((2, 32, 2, legendre...  58 us

profile of v3, /device:TPU:1, one launch (start us, length us, event | category | flops | bytes accessed | tf_op | source)
XLA Modules:
  0.0 58.7 jit_solution(6045099906226477476)
XLA Ops:
  0.0 58.0 %spectrum_at_owner.1 = bf16[2,32,2,513]{3,2,1,0:T(2,128)(2,1)S(1)} custom-call(bf16[2,2,16,3072]{3,2,1,0:T(8,128)(2,1)} %grid_hbm.1, s32[2]{0:T(128)} %slot_hbm.1, f32[4,16,1024]{2,1,0:T(8,128)} %constant.2.clone.seeds_hbm, bf16[513,2,768]{2,1,0:T(2,128)(2,1)} %bitcast.5), custom_call_target="tpu_custom_call" | custom-call | tf_op jit(solution)/shard_map/spectrum_at_owner/pallas_call | solution.py:292
  58.0 0.7 %copy.6 = bf16[1,2,32,2,513]{4,3,2,1,0:T(2,128)(2,1)} copy(bf16[1,2,32,2,513]{4,3,2,1,0:T(2,128)(2,1)S(1)} %bitcast.4) | data formatting | bytes 262656

commit v4 on v3

--- a/solution.py
+++ b/solution.py
@@ -87,7 +87,7 @@
                 )
                 for u in range(4):
                     for part in range(2):
-                        left[u, pl.ds(f * 32 + p * 16, 16), pl.ds(part * INNER + block * 128, 128)] = pieces[u][
+                        left[u, pl.ds(p * 32 + f * 16, 16), pl.ds(part * INNER + block * 128, 128)] = pieces[u][
                             part
                         ].astype(jnp.bfloat16)
 
@@ -97,9 +97,10 @@
         product = jnp.dot(left[u], table[u], preferred_element_type=jnp.float32)
         for s in range(2):
             for r in range(2):
-                waves[s, pl.ds(r * 64, 64), pl.ds(u * 128, 128)] = product[
-                    :, (s * 2 + r) * 128 : (s * 2 + r + 1) * 128
-                ].astype(jnp.bfloat16)
+                for p in range(2):
+                    waves[s, pl.ds(p * 64 + r * 32, 32), pl.ds(u * 128, 128)] = product[
+                        p * 32 : p * 32 + 32, (s * 2 + r) * 128 : (s * 2 + r + 1) * 128
+                    ].astype(jnp.bfloat16)
 
 
 def swap_groups(blocks, shifts):
@@ -116,10 +117,10 @@
     return blocks
 
 
-def pick_slots(c, slot_rows, waves, one_hot, picked, outgoing):
+def pick_slots(c, p, slot_rows, waves, one_hot, picked, put):
     row = lax.broadcasted_iota(jnp.int32, (64, 128), 0) * 8
     for h in range(2):
-        slots = jnp.broadcast_to(slot_rows[c, h : h + 1, :], (64, 128))
+        slots = jnp.broadcast_to(slot_rows[p, c, h : h + 1, :], (64, 128))
         for u in range(4):
             for half in range(2):
                 here = row + wave_rows(u, half)
@@ -127,22 +128,19 @@
                 one_hot[(0, *place)] = jnp.where(here == slots, 1.0, 0.0).astype(jnp.bfloat16)
                 one_hot[(1, *place)] = jnp.where(here == 511 - slots, 1.0, 0.0).astype(jnp.bfloat16)
     for s in range(2):
-        picked[s] = jnp.dot(waves[s], one_hot[s], preferred_element_type=jnp.float32)
+        picked[s] = jnp.dot(waves[s, pl.ds(p * 64, 64), :], one_hot[s], preferred_element_type=jnp.float32)
     for h in range(2):
-        for part in range(2):
-            blocks = [
-                picked[g // 4, pl.ds((g % 2) * 64 + (g // 2 % 2) * 32 + part * 16, 16), pl.ds(h * 128, 128)]
-                for g in range(8)
-            ]
-            for k, block in enumerate(swap_groups(blocks, (1, 2, 64))):
-                outgoing[h * 8 + k, c, pl.ds(part * 16, 16), :] = block.astype(jnp.bfloat16)
-
-
-def gather_fields(c, arrived, turned):
-    for part in range(2):
-        blocks = [arrived[c, f, pl.ds(part * 16, 16), :].astype(jnp.float32) for f in range(FLDS)]
-        for i, block in enumerate(swap_groups(blocks, (4, 8, 16, 32))):
-            turned[c * 16 + i, pl.ds(part * 16, 16), :] = block.astype(jnp.bfloat16)
+        blocks = [
+            picked[g // 4, pl.ds((g % 2) * 32 + (g // 2 % 2) * 16, 16), pl.ds(h * 128, 128)] for g in range(8)
+        ]
+        for k, block in enumerate(swap_groups(blocks, (1, 2, 64))):
+            put(h * 8 + k, block.astype(jnp.bfloat16))
+
+
+def turn_groups(arrived, c, put):
+    blocks = [arrived[c * 16 + f].astype(jnp.float32) for f in range(16)]
+    for i, block in enumerate(swap_groups(blocks, (4, 8, 16, 32))):
+        put(i, block.astype(jnp.bfloat16))
 
 
 def turn_legendre(legendre, by_j):
@@ -183,11 +181,14 @@
 
 def kernel(
     grid_hbm, slot_hbm, seeds_hbm, legendre_hbm, out,
-    grid, slot, seeds, legendre, by_j, flipped, table, left, waves, one_hot, picked, outgoing, arrived, turned, own_column, all_slots, slot_rows, by_row,
-    input_sem, send_list, recv_list, send_lists, recv_lists, send_fld, recv_fld, send_band, recv_band,
+    grid, slot, seeds, legendre, by_j, flipped, table, left, waves, one_hot, picked,
+    own_column, all_slots, slot_rows, by_fld, from_fld, by_band, from_band, by_fld_late, from_fld_late, by_band_late, rows,
+    input_sem, send_list, recv_list, send_lists, recv_lists,
+    send_fld, recv_fld, send_band, recv_band, send_fld_late, recv_fld_late, send_band_late, recv_band_late,
 ):
     band, fld = lax.axis_index("band"), lax.axis_index("fld")
     x, z = band // ZS, band % ZS
+    place = z % 3 * 16 + x * 4 + z // 3
     inputs = (
         pltpu.make_async_copy(seeds_hbm, seeds, input_sem.at[0]),
         pltpu.make_async_copy(grid_hbm, grid, input_sem.at[1]),
@@ -218,11 +219,18 @@
     arrived_at(own_column.at[pl.ds(0, FLDS - 1)], recv_list)
 
     lane = lax.broadcasted_iota(jnp.int32, (1, 128), 1)
+    of_eight, of_sixteen = lane // 64 * 4 + lane % 4, lane // 4 % 16
+    column = [own_column[f] for f in range(FLDS)]
     for h in range(2):
         row = jnp.zeros((1, 128), jnp.int32)
         for k in range(8):
-            row = row + jnp.where(lane // 64 * 4 + lane % 4 == k, own_column[h * 8 + k], 0)
+            row = row + jnp.where(of_eight == k, column[h * 8 + k], 0)
         all_slots[band, pl.ds(h, 1), :] = row
+    row = jnp.zeros((1, 128), jnp.int32)
+    for f in range(FLDS):
+        row = row + jnp.where(of_sixteen == f, column[f], 0)
+    all_slots[band, pl.ds(2, 1), :] = row
+    all_slots[band, pl.ds(3, 1), :] = jnp.zeros((1, 128), jnp.int32)
 
     def lists_start(d):
         pltpu.make_async_remote_copy(
@@ -231,57 +239,108 @@
 
     each(1, BANDS, lists_start)
     long_transform(left, table, waves)
+    inputs[2].wait()
+    turn_legendre(legendre, by_j)
     arrived_at(all_slots.at[pl.ds(0, BANDS - 1)], recv_lists)
-    lanes = lax.broadcasted_iota(jnp.int32, (2, 128), 1)
     for c in range(3):
-        rows = jnp.zeros((2, 128), jnp.int32)
+        members = [(i // 4) * ZS + (i % 4) * 3 + c for i in range(16)]
+        early = jnp.zeros((2, 128), jnp.int32)
         for i in range(16):
-            rows = rows + jnp.where(lanes // 4 % 16 == i, all_slots[(i // 4) * ZS + (i % 4) * 3 + c], 0)
-        slot_rows[c] = rows
-
-    def fld_start(step, c, d):
+            early = early + jnp.where(of_sixteen == i, all_slots[members[i], pl.ds(0, 2), :], 0)
+        slot_rows[0, c] = early
+        for h in range(2):
+            late = jnp.zeros((1, 128), jnp.int32)
+            for k in range(8):
+                late = late + jnp.where(of_eight == k, all_slots[members[h * 8 + k], pl.ds(2, 1), :], 0)
+            slot_rows[1, c, pl.ds(h, 1), :] = late
+
+    def to_fld(source, target, send, recv, step, c, d):
         to = wrap(fld + d, FLDS)
         pltpu.make_async_remote_copy(
-            outgoing.at[to, c], arrived.at[c, fld], send_fld, recv_fld.at[step], device_id={"fld": to}
+            source.at[to, c], target.at[c * 16 + fld], send, recv.at[step], device_id={"fld": to}
+        ).start()
+
+    def to_band(step, o):
+        to_x, to_z = wrap(x + o // 4, 4), wrap(z + step + 3 * (o % 4), ZS)
+        return to_z % 3 * 16 + to_x * 4 + to_z // 3, {"band": to_x * ZS + to_z}
+
+    def band_start(step, o):
+        i, to = to_band(step, o)
+        pltpu.make_async_remote_copy(
+            by_band.at[i], from_band.at[place], send_band, recv_band.at[step], device_id=to
+        ).start()
+
+    def band_late_start(step, o):
+        i, to = to_band(step, o)
+        pltpu.make_async_remote_copy(
+            by_band_late.at[i], rows.at[0, band], send_band_late, recv_band_late, device_id=to
         ).start()
 
     def chunk_out(step, carry):
         c = (z + step) % 3
-        pick_slots(c, slot_rows, waves, one_hot, picked, outgoing)
-        each(1, FLDS, lambda d: fld_start(step, c, d))
-        arrived[c, fld] = outgoing[fld, c]
+
+        def put_band(i, block):
+            by_band[c * 16 + i] = block
+
+        def put_fld(f, block):
+            by_fld[f, c] = block
+
+        pick_slots(c, 1, slot_rows, waves, one_hot, picked, put_band)
+        each(jnp.where(step == 0, 1, 0), 16, lambda o: band_start(step, o))
+        pick_slots(c, 0, slot_rows, waves, one_hot, picked, put_fld)
+        each(1, FLDS, lambda d: to_fld(by_fld, from_fld, send_fld, recv_fld, step, c, d))
+        from_fld[c * 16 + fld] = by_fld[fld, c]
         return carry
 
     lax.fori_loop(0, 3, chunk_out, 0)
-
-    def band_start(step, o):
-        to_x, to_z = wrap(x + o // 4, 4), wrap(z + step + 3 * (o % 4), ZS)
-        pltpu.make_async_remote_copy(
-            turned.at[(to_z % 3) * 16 + to_x * 4 + to_z // 3], by_row.at[band], send_band, recv_band,
-            device_id={"band": to_x * ZS + to_z},
-        ).start()
+    from_band[place] = by_band[place]
 
     for step in range(3):
         c = (z + step) % 3
-        arrived_at(arrived.at[c, pl.ds(0, FLDS - 1)], recv_fld.at[step])
-        gather_fields(c, arrived, turned)
-        each(0 if step else 1, 16, lambda o: band_start(step, o))
-        if step == 0:
-            by_row[band] = turned[c * 16 + x * 4 + z // 3]
-    inputs[2].wait()
-    turn_legendre(legendre, by_j)
+
+        def put_band_late(i, block, c=c):
+            by_band_late[c * 16 + i] = block
+
+        arrived_at(from_fld.at[pl.ds(c * 16, FLDS - 1)], recv_fld.at[step])
+        turn_groups(from_fld, c, put_band_late)
+        each(0 if step else 1, 16, lambda o, step=step: band_late_start(step, o))
+    rows[0, band] = by_band_late[place]
+
+    for step in range(3):
+        c = (z + 3 - step) % 3
+
+        def put_fld_late(f, block, c=c):
+            by_fld_late[f, c] = block
+
+        arrived_at(from_band.at[pl.ds(c * 16, 16 if step else 15)], recv_band.at[step])
+        turn_groups(from_band, c, put_fld_late)
+        each(1, FLDS, lambda d, step=step, c=c: to_fld(by_fld_late, from_fld_late, send_fld_late, recv_fld_late, step, c, d))
+        from_fld_late[c * 16 + fld] = by_fld_late[fld, c]
+
+    def finish(p):
+        for block in range(6):
+            piece = rows[p, pl.ds(block * 8, 8)].reshape(128, 128)
+            flipped[p, :, pl.ds(block * 128, 128)] = piece.T
+        products = jnp.dot(flipped[p], by_j[p], preferred_element_type=jnp.float32)
+        out[p] = choose_columns(p, slot[0], products).astype(jnp.bfloat16).reshape(32, 2, 640)[:, :, :513]
+
     arrived_at(own_column.at[pl.ds(0, FLDS - 1)], send_list)
     arrived_at(all_slots.at[pl.ds(0, BANDS - 1)], send_lists)
-    arrived_at(outgoing.at[pl.ds(0, FLDS - 1)], send_fld)
-    arrived_at(by_row.at[pl.ds(0, BANDS - 1)], recv_band)
-    for p in range(2):
-        for block in range(6):
-            rows = by_row[pl.ds(block * 8, 8), pl.ds(p * 16, 16), :].reshape(128, 128)
-            flipped[p, :, pl.ds(block * 128, 128)] = rows.T
-    for p in range(2):
-        products = jnp.dot(flipped[p], by_j[p], preferred_element_type=jnp.float32)
-        out[p] = choose_columns(p, slot[0], products).astype(jnp.bfloat16).reshape(32, 2, 640)[:, :, :513]
-    arrived_at(turned.at[pl.ds(0, BANDS - 1)], send_band)
+    arrived_at(by_fld.at[pl.ds(0, FLDS - 1)], send_fld)
+    arrived_at(by_band.at[pl.ds(0, BANDS - 1)], send_band)
+    for step in range(3):
+        c = (z + 3 - step) % 3
+
+        def put_row(i, block, c=c):
+            rows[1, (i // 4) * ZS + (i % 4) * 3 + c] = block
+
+        arrived_at(from_fld_late.at[pl.ds(c * 16, FLDS - 1)], recv_fld_late.at[step])
+        turn_groups(from_fld_late, c, put_row)
+    finish(1)
+    arrived_at(rows.at[0, pl.ds(0, BANDS - 1)], recv_band_late)
+    finish(0)
+    arrived_at(by_fld_late.at[pl.ds(0, FLDS - 1)], send_fld_late)
+    arrived_at(by_band_late.at[pl.ds(0, BANDS - 1)], send_band_late)
 
 
 def spectrum_at_owner(grid_fields, slot_wave, legendre):
@@ -305,15 +364,20 @@
             pltpu.VMEM((4, 64, 768), bf16),
             pltpu.VMEM((2, 128, 512), bf16),
             pltpu.VMEM((2, 512, 256), bf16),
-            pltpu.VMEM((2, 128, 256), f32),
-            pltpu.VMEM((FLDS, 3, 32, 128), bf16),
-            pltpu.VMEM((3, FLDS, 32, 128), bf16),
-            pltpu.VMEM((BANDS, 32, 128), bf16),
+            pltpu.VMEM((2, 64, 256), f32),
             pltpu.VMEM((FLDS, 1, 128), i32),
-            pltpu.VMEM((BANDS, 2, 128), i32),
-            pltpu.VMEM((3, 2, 128), i32),
-            pltpu.VMEM((BANDS, 32, 128), bf16),
-            dma((4,)), dma, dma, dma, dma, dma, dma((3,)), dma, dma,
+            pltpu.VMEM((BANDS, 4, 128), i32),
+            pltpu.VMEM((2, 3, 2, 128), i32),
+            pltpu.VMEM((FLDS, 3, 16, 128), bf16),
+            pltpu.VMEM((48, 16, 128), bf16),
+            pltpu.VMEM((48, 16, 128), bf16),
+            pltpu.VMEM((48, 16, 128), bf16),
+            pltpu.VMEM((FLDS, 3, 16, 128), bf16),
+            pltpu.VMEM((48, 16, 128), bf16),
+            pltpu.VMEM((48, 16, 128), bf16),
+            pltpu.VMEM((2, BANDS, 16, 128), bf16),
+            dma((4,)), dma, dma, dma, dma,
+            dma, dma((3,)), dma, dma((3,)), dma, dma((3,)), dma, dma,
         ],
         compiler_params=pltpu.CompilerParams(
             collective_id=0, has_side_effects=True, vmem_limit_bytes=24 * 1024 * 1024

time: 58.8 us -> 55.1 us (0.937)
  Pallas kernels: 58 us -> 54.3 us
    pallas_call x1, Pallas kernels: 58 us -> 54.3 us  [spectrum_at_owner(): pl.pallas_call(kernel, out_shape=jax.ShapeDtypeStruct((2, 32, 2, legendre...]
where the time goes in v4:
time: 55.1 us; the launch traced here: 55 us
  Pallas kernels  54.3 us (99%)
  local copies, waits for them, and re-layouts  0.67 us (1%)
    pallas_call x1, Pallas kernels, spectrum_at_owner(): pl.pallas_call(kernel, out_shape=jax.ShapeDtypeStruct((2, 32, 2, legendre...  54.3 us

profile of v4, /device:TPU:1, one launch (start us, length us, event | category | flops | bytes accessed | tf_op | source)
XLA Modules:
  0.0 55.0 jit_solution(507134995139934147)
XLA Ops:
  0.0 54.3 %spectrum_at_owner.1 = bf16[2,32,2,513]{3,2,1,0:T(2,128)(2,1)S(1)} custom-call(bf16[2,2,16,3072]{3,2,1,0:T(8,128)(2,1)} %grid_hbm.1, s32[2]{0:T(128)} %slot_hbm.1, f32[4,16,1024]{2,1,0:T(8,128)} %constant.2.clone.seeds_hbm, bf16[513,2,768]{2,1,0:T(2,128)(2,1)} %bitcast.5), custom_call_target="tpu_custom_call" | custom-call | tf_op jit(solution)/shard_map/spectrum_at_owner/pallas_call | solution.py:351
  54.3 0.7 %copy.6 = bf16[1,2,32,2,513]{4,3,2,1,0:T(2,128)(2,1)} copy(bf16[1,2,32,2,513]{4,3,2,1,0:T(2,128)(2,1)S(1)} %bitcast.4) | data formatting | bytes 262656

commit v5 on v4

--- a/solution.py
+++ b/solution.py
@@ -1,3 +1,4 @@
+import functools
 import math
 
 import jax
@@ -117,24 +118,28 @@
     return blocks
 
 
-def pick_slots(c, p, slot_rows, waves, one_hot, picked, put):
+def pick_slots(c, slot_rows, waves, one_hot, picked, puts):
     row = lax.broadcasted_iota(jnp.int32, (64, 128), 0) * 8
-    for h in range(2):
-        slots = jnp.broadcast_to(slot_rows[p, c, h : h + 1, :], (64, 128))
-        for u in range(4):
-            for half in range(2):
-                here = row + wave_rows(u, half)
-                place = (pl.ds(u * 128 + half * 64, 64), pl.ds(h * 128, 128))
-                one_hot[(0, *place)] = jnp.where(here == slots, 1.0, 0.0).astype(jnp.bfloat16)
-                one_hot[(1, *place)] = jnp.where(here == 511 - slots, 1.0, 0.0).astype(jnp.bfloat16)
-    for s in range(2):
-        picked[s] = jnp.dot(waves[s, pl.ds(p * 64, 64), :], one_hot[s], preferred_element_type=jnp.float32)
-    for h in range(2):
-        blocks = [
-            picked[g // 4, pl.ds((g % 2) * 32 + (g // 2 % 2) * 16, 16), pl.ds(h * 128, 128)] for g in range(8)
-        ]
-        for k, block in enumerate(swap_groups(blocks, (1, 2, 64))):
-            put(h * 8 + k, block.astype(jnp.bfloat16))
+    for p in (1, 0):
+        for h in range(2):
+            slots = jnp.broadcast_to(slot_rows[p, c, h : h + 1, :], (64, 128))
+            for u in range(4):
+                for half in range(2):
+                    here = row + wave_rows(u, half)
+                    place = (pl.ds(u * 128 + half * 64, 64), pl.ds(h * 128, 128))
+                    one_hot[(p, 0, *place)] = jnp.where(here == slots, 1.0, 0.0).astype(jnp.bfloat16)
+                    one_hot[(p, 1, *place)] = jnp.where(here == 511 - slots, 1.0, 0.0).astype(jnp.bfloat16)
+        for s in range(2):
+            picked[p, s] = jnp.dot(
+                waves[s, pl.ds(p * 64, 64), :], one_hot[p, s], preferred_element_type=jnp.float32
+            )
+    for p in (1, 0):
+        for h in range(2):
+            blocks = [
+                picked[p, g // 4, pl.ds((g % 2) * 32 + (g // 2 % 2) * 16, 16), pl.ds(h * 128, 128)] for g in range(8)
+            ]
+            for k, block in enumerate(swap_groups(blocks, (1, 2, 64))):
+                puts[p](h * 8 + k, block.astype(jnp.bfloat16))
 
 
 def turn_groups(arrived, c, put):
@@ -173,10 +178,6 @@
 
 def arrived_at(ref, semaphore):
     pltpu.make_async_copy(ref, ref, semaphore).wait()
-
-
-def each(first, last, act):
-    lax.fori_loop(first, last, lambda k, carry: (act(k), carry)[1], 0)
 
 
 def kernel(
@@ -197,21 +198,27 @@
     own_slot = pltpu.make_async_copy(slot_hbm, slot, input_sem.at[3])
     own_slot.start()
 
+    all_x = [wrap(x + dx, 4) for dx in range(4)]
+    all_z = [wrap(z + dz, ZS) for dz in range(ZS)]
+    hops = sorted(((min(dx, 4 - dx) + min(dz, ZS - dz), dx, dz) for dx in range(4) for dz in range(ZS)), reverse=True)
+    band_peers = [{"band": all_x[dx] * ZS + all_z[dz]} for far, dx, dz in hops if far]
+    fld_peers = [{"fld": wrap(fld + d, FLDS)} for d in sorted(range(1, FLDS), key=lambda d: -min(d, FLDS - d))]
+
     barrier = pltpu.get_barrier_semaphore()
-    each(1, BANDS, lambda d: pl.semaphore_signal(barrier, inc=1, device_id={"band": wrap(band + d, BANDS)}))
-    each(1, FLDS, lambda d: pl.semaphore_signal(barrier, inc=1, device_id={"fld": wrap(fld + d, FLDS)}))
+    for to in band_peers:
+        pl.semaphore_signal(barrier, inc=1, device_id=to)
+    for to in fld_peers:
+        pl.semaphore_signal(barrier, inc=1, device_id=to)
     for copy in inputs:
         copy.start()
     own_slot.wait()
     own_column[fld] = jnp.full((1, 128), slot[0], jnp.int32)
     pl.semaphore_wait(barrier, FLDS - 1 + BANDS - 1)
 
-    def list_start(d):
+    for to in fld_peers:
         pltpu.make_async_remote_copy(
-            own_column.at[fld], own_column.at[fld], send_list, recv_list, device_id={"fld": wrap(fld + d, FLDS)}
+            own_column.at[fld], own_column.at[fld], send_list, recv_list, device_id=to
         ).start()
-
-    each(1, FLDS, list_start)
     for copy in inputs[:2]:
         copy.wait()
     make_table(seeds, table)
@@ -232,12 +239,10 @@
     all_slots[band, pl.ds(2, 1), :] = row
     all_slots[band, pl.ds(3, 1), :] = jnp.zeros((1, 128), jnp.int32)
 
-    def lists_start(d):
+    for to in band_peers:
         pltpu.make_async_remote_copy(
-            all_slots.at[band], all_slots.at[band], send_lists, recv_lists, device_id={"band": wrap(band + d, BANDS)}
+            all_slots.at[band], all_slots.at[band], send_lists, recv_lists, device_id=to
         ).start()
-
-    each(1, BANDS, lists_start)
     long_transform(left, table, waves)
     inputs[2].wait()
     turn_legendre(legendre, by_j)
@@ -254,27 +259,29 @@
                 late = late + jnp.where(of_eight == k, all_slots[members[h * 8 + k], pl.ds(2, 1), :], 0)
             slot_rows[1, c, pl.ds(h, 1), :] = late
 
-    def to_fld(source, target, send, recv, step, c, d):
-        to = wrap(fld + d, FLDS)
-        pltpu.make_async_remote_copy(
-            source.at[to, c], target.at[c * 16 + fld], send, recv.at[step], device_id={"fld": to}
-        ).start()
-
-    def to_band(step, o):
-        to_x, to_z = wrap(x + o // 4, 4), wrap(z + step + 3 * (o % 4), ZS)
-        return to_z % 3 * 16 + to_x * 4 + to_z // 3, {"band": to_x * ZS + to_z}
-
-    def band_start(step, o):
-        i, to = to_band(step, o)
-        pltpu.make_async_remote_copy(
-            by_band.at[i], from_band.at[place], send_band, recv_band.at[step], device_id=to
-        ).start()
-
-    def band_late_start(step, o):
-        i, to = to_band(step, o)
-        pltpu.make_async_remote_copy(
-            by_band_late.at[i], rows.at[0, band], send_band_late, recv_band_late, device_id=to
-        ).start()
+    def to_fld(source, target, send, recv, step, c):
+        for to in fld_peers:
+            pltpu.make_async_remote_copy(
+                source.at[to["fld"], c], target.at[c * 16 + fld], send, recv.at[step], device_id=to
+            ).start()
+
+    def to_band(step, send):
+        c = wrap(z % 3 + step, 3)
+        to_z = [wrap(z + step + 3 * k, ZS) for k in range(4)]
+        high = [(at - c) // 3 for at in to_z]
+        for k in range(4):
+            for dx in range(4):
+                act = functools.partial(
+                    send, c * 16 + all_x[dx] * 4 + high[k], {"band": all_x[dx] * ZS + to_z[k]}
+                )
+                if k == dx == 0:
+                    if isinstance(step, int):
+                        if step:
+                            act()
+                    else:
+                        pl.when(step > 0)(act)
+                else:
+                    act()
 
     def chunk_out(step, carry):
         c = (z + step) % 3
@@ -285,37 +292,48 @@
         def put_fld(f, block):
             by_fld[f, c] = block
 
-        pick_slots(c, 1, slot_rows, waves, one_hot, picked, put_band)
-        each(jnp.where(step == 0, 1, 0), 16, lambda o: band_start(step, o))
-        pick_slots(c, 0, slot_rows, waves, one_hot, picked, put_fld)
-        each(1, FLDS, lambda d: to_fld(by_fld, from_fld, send_fld, recv_fld, step, c, d))
+        pick_slots(c, slot_rows, waves, one_hot, picked, (put_fld, put_band))
+        to_band(step, lambda i, to: pltpu.make_async_remote_copy(
+            by_band.at[i], from_band.at[place], send_band, recv_band.at[step], device_id=to
+        ).start())
+        to_fld(by_fld, from_fld, send_fld, recv_fld, step, c)
         from_fld[c * 16 + fld] = by_fld[fld, c]
         return carry
 
     lax.fori_loop(0, 3, chunk_out, 0)
     from_band[place] = by_band[place]
 
-    for step in range(3):
+    def middle_fld(step):
         c = (z + step) % 3
 
-        def put_band_late(i, block, c=c):
+        def put_band_late(i, block):
             by_band_late[c * 16 + i] = block
 
         arrived_at(from_fld.at[pl.ds(c * 16, FLDS - 1)], recv_fld.at[step])
         turn_groups(from_fld, c, put_band_late)
-        each(0 if step else 1, 16, lambda o, step=step: band_late_start(step, o))
-    rows[0, band] = by_band_late[place]
-
-    for step in range(3):
+        to_band(step, lambda i, to: pltpu.make_async_remote_copy(
+            by_band_late.at[i], rows.at[0, band], send_band_late, recv_band_late, device_id=to
+        ).start())
+        if step == 0:
+            rows[0, band] = by_band_late[place]
+
+    def middle_band(step):
         c = (z + 3 - step) % 3
 
-        def put_fld_late(f, block, c=c):
+        def put_fld_late(f, block):
             by_fld_late[f, c] = block
 
         arrived_at(from_band.at[pl.ds(c * 16, 16 if step else 15)], recv_band.at[step])
         turn_groups(from_band, c, put_fld_late)
-        each(1, FLDS, lambda d, step=step, c=c: to_fld(by_fld_late, from_fld_late, send_fld_late, recv_fld_late, step, c, d))
+        to_fld(by_fld_late, from_fld_late, send_fld_late, recv_fld_late, step, c)
         from_fld_late[c * 16 + fld] = by_fld_late[fld, c]
+
+    middle_fld(0)
+    middle_fld(1)
+    middle_band(0)
+    middle_fld(2)
+    middle_band(1)
+    middle_band(2)
 
     def finish(p):
         for block in range(6):
@@ -328,17 +346,21 @@
     arrived_at(all_slots.at[pl.ds(0, BANDS - 1)], send_lists)
     arrived_at(by_fld.at[pl.ds(0, FLDS - 1)], send_fld)
     arrived_at(by_band.at[pl.ds(0, BANDS - 1)], send_band)
-    for step in range(3):
+    def last_fld(step):
         c = (z + 3 - step) % 3
 
-        def put_row(i, block, c=c):
+        def put_row(i, block):
             rows[1, (i // 4) * ZS + (i % 4) * 3 + c] = block
 
         arrived_at(from_fld_late.at[pl.ds(c * 16, FLDS - 1)], recv_fld_late.at[step])
         turn_groups(from_fld_late, c, put_row)
-    finish(1)
+
+    last_fld(0)
+    last_fld(1)
     arrived_at(rows.at[0, pl.ds(0, BANDS - 1)], recv_band_late)
     finish(0)
+    last_fld(2)
+    finish(1)
     arrived_at(by_fld_late.at[pl.ds(0, FLDS - 1)], send_fld_late)
     arrived_at(by_band_late.at[pl.ds(0, BANDS - 1)], send_band_late)
 
@@ -363,8 +385,8 @@
             pltpu.VMEM((4, 768, 512), bf16),
             pltpu.VMEM((4, 64, 768), bf16),
             pltpu.VMEM((2, 128, 512), bf16),
-            pltpu.VMEM((2, 512, 256), bf16),
-            pltpu.VMEM((2, 64, 256), f32),
+            pltpu.VMEM((2, 2, 512, 256), bf16),
+            pltpu.VMEM((2, 2, 64, 256), f32),
             pltpu.VMEM((FLDS, 1, 128), i32),
             pltpu.VMEM((BANDS, 4, 128), i32),
             pltpu.VMEM((2, 3, 2, 128), i32),

time: 55.1 us -> 51.4 us (0.933)
  Pallas kernels: 54.3 us -> 50.6 us
    pallas_call x1, Pallas kernels: 54.3 us -> 50.6 us  [spectrum_at_owner(): pl.pallas_call(kernel, out_shape=jax.ShapeDtypeStruct((2, 32, 2, legendre...]
where the time goes in v5:
time: 51.4 us; the launch traced here: 51.2 us
  Pallas kernels  50.6 us (98%)
  local copies, waits for them, and re-layouts  0.67 us (1%)
    pallas_call x1, Pallas kernels, spectrum_at_owner(): pl.pallas_call(kernel, out_shape=jax.ShapeDtypeStruct((2, 32, 2, legendre...  50.6 us

profile of v5, /device:TPU:1, one launch (start us, length us, event | category | flops | bytes accessed | tf_op | source)
XLA Modules:
  0.0 51.2 jit_solution(2616414998142511424)
XLA Ops:
  0.0 50.6 %spectrum_at_owner.1 = bf16[2,32,2,513]{3,2,1,0:T(2,128)(2,1)S(1)} custom-call(bf16[2,2,16,3072]{3,2,1,0:T(8,128)(2,1)} %grid_hbm.1, s32[2]{0:T(128)} %slot_hbm.1, f32[4,16,1024]{2,1,0:T(8,128)} %constant.2.clone.seeds_hbm, bf16[513,2,768]{2,1,0:T(2,128)(2,1)} %bitcast.5), custom_call_target="tpu_custom_call" | custom-call | tf_op jit(solution)/shard_map/spectrum_at_owner/pallas_call | solution.py:373
  50.6 0.7 %copy.6 = bf16[1,2,32,2,513]{4,3,2,1,0:T(2,128)(2,1)} copy(bf16[1,2,32,2,513]{4,3,2,1,0:T(2,128)(2,1)S(1)} %bitcast.4) | data formatting | bytes 262656

commit v6 on v5

--- a/solution.py
+++ b/solution.py
@@ -161,7 +161,11 @@
                 piece = values[:, p, :]
                 if c == 4:
                     piece = jnp.where(first, jnp.broadcast_to(piece, (128, 128)), 0.0)
-                by_j[p, at, pl.ds(c * 128, 128)] = piece.astype(jnp.bfloat16).T
+                piece = piece.astype(jnp.bfloat16).T
+                for k in range(8):
+                    row, depth = divmod(block * 8 + k, ZS)
+                    to = (depth % 3 * 16 + row * 4 + depth // 3) * 16
+                    by_j[p, pl.ds(to, 16), pl.ds(c * 128, 128)] = piece[k * 16 : k * 16 + 16]
 
 
 def choose_columns(p, wave, products):
@@ -182,7 +186,7 @@
 
 def kernel(
     grid_hbm, slot_hbm, seeds_hbm, legendre_hbm, out,
-    grid, slot, seeds, legendre, by_j, flipped, table, left, waves, one_hot, picked,
+    grid, slot, seeds, legendre, by_j, flipped, total, table, left, waves, one_hot, picked,
     own_column, all_slots, slot_rows, by_fld, from_fld, by_band, from_band, by_fld_late, from_fld_late, by_band_late, rows,
     input_sem, send_list, recv_list, send_lists, recv_lists,
     send_fld, recv_fld, send_band, recv_band, send_fld_late, recv_fld_late, send_band_late, recv_band_late,
@@ -265,23 +269,22 @@
                 source.at[to["fld"], c], target.at[c * 16 + fld], send, recv.at[step], device_id=to
             ).start()
 
+    far_first = sorted(
+        ((min(dx, 4 - dx) + (3 * k + 1 if k < 2 else 11 - 3 * k), k, dx) for k in range(4) for dx in range(4)), reverse=True
+    )
+
     def to_band(step, send):
         c = wrap(z % 3 + step, 3)
         to_z = [wrap(z + step + 3 * k, ZS) for k in range(4)]
         high = [(at - c) // 3 for at in to_z]
-        for k in range(4):
-            for dx in range(4):
-                act = functools.partial(
-                    send, c * 16 + all_x[dx] * 4 + high[k], {"band": all_x[dx] * ZS + to_z[k]}
-                )
-                if k == dx == 0:
-                    if isinstance(step, int):
-                        if step:
-                            act()
-                    else:
-                        pl.when(step > 0)(act)
-                else:
-                    act()
+        for far, k, dx in far_first:
+            act = functools.partial(send, c * 16 + all_x[dx] * 4 + high[k], {"band": all_x[dx] * ZS + to_z[k]})
+            if k or dx:
+                act()
+            elif not isinstance(step, int):
+                pl.when(step > 0)(act)
+            elif step:
+                act()
 
     def chunk_out(step, carry):
         c = (z + step) % 3
@@ -312,10 +315,10 @@
         arrived_at(from_fld.at[pl.ds(c * 16, FLDS - 1)], recv_fld.at[step])
         turn_groups(from_fld, c, put_band_late)
         to_band(step, lambda i, to: pltpu.make_async_remote_copy(
-            by_band_late.at[i], rows.at[0, band], send_band_late, recv_band_late, device_id=to
+            by_band_late.at[i], rows.at[0, place], send_band_late, recv_band_late.at[step], device_id=to
         ).start())
         if step == 0:
-            rows[0, band] = by_band_late[place]
+            rows[0, place] = by_band_late[place]
 
     def middle_band(step):
         c = (z + 3 - step) % 3
@@ -330,17 +333,23 @@
 
     middle_fld(0)
     middle_fld(1)
+    middle_fld(2)
     middle_band(0)
-    middle_fld(2)
     middle_band(1)
     middle_band(2)
 
-    def finish(p):
-        for block in range(6):
-            piece = rows[p, pl.ds(block * 8, 8)].reshape(128, 128)
-            flipped[p, :, pl.ds(block * 128, 128)] = piece.T
-        products = jnp.dot(flipped[p], by_j[p], preferred_element_type=jnp.float32)
-        out[p] = choose_columns(p, slot[0], products).astype(jnp.bfloat16).reshape(32, 2, 640)[:, :, :513]
+    def add_chunk(p, c, step):
+        for half in range(2):
+            piece = rows[p, pl.ds(c * 16 + half * 8, 8)].reshape(128, 128)
+            flipped[p, :, pl.ds(half * 128, 128)] = piece.T
+        deep = pl.ds(pl.multiple_of(c * 256, 256), 256)
+        products = jnp.dot(flipped[p], by_j[p, deep, :], preferred_element_type=jnp.float32)
+        if step:
+            products = total[p] + products
+        if step < 2:
+            total[p] = products
+        else:
+            out[p] = choose_columns(p, slot[0], products).astype(jnp.bfloat16).reshape(32, 2, 640)[:, :, :513]
 
     arrived_at(own_column.at[pl.ds(0, FLDS - 1)], send_list)
     arrived_at(all_slots.at[pl.ds(0, BANDS - 1)], send_lists)
@@ -350,17 +359,23 @@
         c = (z + 3 - step) % 3
 
         def put_row(i, block):
-            rows[1, (i // 4) * ZS + (i % 4) * 3 + c] = block
+            rows[1, c * 16 + i] = block
 
         arrived_at(from_fld_late.at[pl.ds(c * 16, FLDS - 1)], recv_fld_late.at[step])
         turn_groups(from_fld_late, c, put_row)
+        add_chunk(1, c, step)
+
+    def last_band(step):
+        c = (z + 3 - step) % 3
+        arrived_at(rows.at[0, pl.ds(c * 16, 16 if step else 15)], recv_band_late.at[step])
+        add_chunk(0, c, step)
 
     last_fld(0)
+    last_band(0)
     last_fld(1)
-    arrived_at(rows.at[0, pl.ds(0, BANDS - 1)], recv_band_late)
-    finish(0)
+    last_band(1)
     last_fld(2)
-    finish(1)
+    last_band(2)
     arrived_at(by_fld_late.at[pl.ds(0, FLDS - 1)], send_fld_late)
     arrived_at(by_band_late.at[pl.ds(0, BANDS - 1)], send_band_late)
 
@@ -381,7 +396,8 @@
             pltpu.VMEM((4, STEPS, 1024), f32),
             pltpu.VMEM(legendre.shape, bf16),
             pltpu.VMEM((2, 768, 640), bf16),
-            pltpu.VMEM((2, 128, 768), bf16),
+            pltpu.VMEM((2, 128, 256), bf16),
+            pltpu.VMEM((2, 128, 640), f32),
             pltpu.VMEM((4, 768, 512), bf16),
             pltpu.VMEM((4, 64, 768), bf16),
             pltpu.VMEM((2, 128, 512), bf16),
@@ -399,7 +415,7 @@
             pltpu.VMEM((48, 16, 128), bf16),
             pltpu.VMEM((2, BANDS, 16, 128), bf16),
             dma((4,)), dma, dma, dma, dma,
-            dma, dma((3,)), dma, dma((3,)), dma, dma((3,)), dma, dma,
+            dma, dma((3,)), dma, dma((3,)), dma, dma((3,)), dma, dma((3,)),
         ],
         compiler_params=pltpu.CompilerParams(
             collective_id=0, has_side_effects=True, vmem_limit_bytes=24 * 1024 * 1024

time: 51.4 us -> 50.9 us (level)
    pallas_call x1, Pallas kernels: 50.6 us -> 50.1 us  [spectrum_at_owner(): pl.pallas_call(kernel, out_shape=jax.ShapeDtypeStruct((2, 32, 2, legendre...]
where the time goes in v6:
time: 50.9 us; the launch traced here: 50.7 us
  Pallas kernels  50.1 us (98%)
  local copies, waits for them, and re-layouts  0.67 us (1%)
    pallas_call x1, Pallas kernels, spectrum_at_owner(): pl.pallas_call(kernel, out_shape=jax.ShapeDtypeStruct((2, 32, 2, legendre...  50.1 us

profile of v6, /device:TPU:1, one launch (start us, length us, event | category | flops | bytes accessed | tf_op | source)
XLA Modules:
  0.0 50.7 jit_solution(12923782265944727748)
XLA Ops:
  0.0 50.1 %spectrum_at_owner.1 = bf16[2,32,2,513]{3,2,1,0:T(2,128)(2,1)S(1)} custom-call(bf16[2,2,16,3072]{3,2,1,0:T(8,128)(2,1)} %grid_hbm.1, s32[2]{0:T(128)} %slot_hbm.1, f32[4,16,1024]{2,1,0:T(8,128)} %constant.2.clone.seeds_hbm, bf16[513,2,768]{2,1,0:T(2,128)(2,1)} %bitcast.5), custom_call_target="tpu_custom_call" | custom-call | tf_op jit(solution)/shard_map/spectrum_at_owner/pallas_call | solution.py:388
  50.1 0.7 %copy.6 = bf16[1,2,32,2,513]{4,3,2,1,0:T(2,128)(2,1)} copy(bf16[1,2,32,2,513]{4,3,2,1,0:T(2,128)(2,1)S(1)} %bitcast.4) | data formatting | bytes 262656
